TPU v7x, 256 devices: a whole 4x4x8 slice. The times are simulated.
256 devices in a mesh: blk: 32 (over z_hi, y, core), head: 8 (over z_lo, x).
Axes of the slice: x: 4, y: 4, z: 8 (z_hi: 4, z_lo: 2; z = z_hi * 2 + z_lo), core: 2. Of those that a mesh axis runs over, the one named last changes fastest.
Arguments:
- query: bfloat16 [32768, 3072], P(('blk', 'head')), may hold values from -6 to 6
- keys: bfloat16 [32768, 3072], P(('blk', 'head')), may hold values from -6 to 6
- values: bfloat16 [32768, 3072], P(('blk', 'head')), may hold values from -6 to 6
- cotangent: bfloat16 [32768, 3072], P(('blk', 'head')), may hold values from -6 to 6
- kv_tiles: int32 [24, 256, 9], P('head'), may hold values from 0 to 255, as said below
Outputs:
- attended: bfloat16 [32768, 3072], P(('blk', 'head'))
- d_query: bfloat16 [32768, 3072], P(('blk', 'head'))
- d_keys: bfloat16 [32768, 3072], P(('blk', 'head'))
- d_values: bfloat16 [32768, 3072], P(('blk', 'head'))
Inputs may be any that keep to these rules, and one draw needn't show every extreme that they name: `kv_tiles`: the 9 entries of a row are distinct; the first 2 entries are the same in every row of one head (that head's global tiles); every other entry lies within 8 tiles of the row's query tile and is not a global tile of that head.
All inputs are finite; a program needn't handle non-finite values.
Results may differ from a plain program's by a relative error of at most 0.017.
Values may be sent and summed in bfloat16 or wider, within the bound.
A program may use at most 192 MiB of HBM per device.

v0:
```python
import jax
import jax.numpy as jnp
from jax import lax
from jax.sharding import PartitionSpec as P

HD = 128
TILE = 128
GLOBALS = 2
HALF = 8


def passed_along(block, axis, distance):
    devices = range(lax.axis_size(axis))
    route = [(i - distance, i) for i in devices if i - distance in devices]
    return lax.ppermute(block, axis, route)


def split_heads(field, count):
    heads = field.shape[1] // HD
    return field.reshape(count, TILE, heads, HD).transpose(2, 0, 1, 3)


def merge_heads(field):
    heads = field.shape[0]
    count = field.shape[1]
    return field.transpose(1, 2, 0, 3).reshape(count * TILE, heads * HD)


def recompute_probs(queries, chosen_keys, log_total):
    scale = HD ** (-0.5)
    scores = (
        jnp.einsum("tqd,tskd->tqsk", queries, chosen_keys, preferred_element_type=jnp.float32)
        * scale
    )
    return jnp.exp(scores - log_total)


def attend_forward(item):
    queries, pool_keys, pool_values, pool_index = item
    scale = HD ** (-0.5)
    chosen_keys = jnp.take(pool_keys, pool_index, axis=0)
    chosen_values = jnp.take(pool_values, pool_index, axis=0)
    scores = (
        jnp.einsum("tqd,tskd->tqsk", queries, chosen_keys, preferred_element_type=jnp.float32)
        * scale
    )
    peak = jnp.max(scores, axis=(2, 3), keepdims=True)
    log_total = peak + jnp.log(jnp.sum(jnp.exp(scores - peak), axis=(2, 3), keepdims=True))
    weights = jnp.exp(scores - log_total).astype(jnp.bfloat16)
    attended = jnp.einsum(
        "tqsk,tskd->tqd", weights, chosen_values, preferred_element_type=jnp.float32
    )
    return (attended.astype(jnp.bfloat16), log_total)


def attend_backward(item):
    queries, pool_keys, pool_values, grad_out, attended, log_total, pool_index = item
    scale = HD ** (-0.5)
    chosen_keys = jnp.take(pool_keys, pool_index, axis=0)
    chosen_values = jnp.take(pool_values, pool_index, axis=0)
    probs = recompute_probs(queries, chosen_keys, log_total)
    weights = probs.astype(jnp.bfloat16)
    delta = jnp.sum(grad_out.astype(jnp.float32) * attended.astype(jnp.float32), axis=-1)
    grad_probs = jnp.einsum(
        "tqd,tskd->tqsk", grad_out, chosen_values, preferred_element_type=jnp.float32
    )
    grad_scores = (probs * (grad_probs - delta[:, :, None, None])).astype(jnp.bfloat16)
    grad_query = (
        jnp.einsum("tqsk,tskd->tqd", grad_scores, chosen_keys, preferred_element_type=jnp.float32)
        * scale
    )
    key_slots = (
        jnp.einsum("tqsk,tqd->tskd", grad_scores, queries, preferred_element_type=jnp.float32)
        * scale
    )
    value_slots = jnp.einsum(
        "tqsk,tqd->tskd", weights, grad_out, preferred_element_type=jnp.float32
    )
    slot_count = pool_index.shape[0] * pool_index.shape[1]
    places = (
        pool_index.reshape(-1)[:, None] == jnp.arange(pool_keys.shape[0], dtype=jnp.int32)[None, :]
    ).astype(jnp.float32)
    key_pool = jnp.einsum(
        "sp,skd->pkd",
        places,
        key_slots.reshape(slot_count, TILE, HD),
        precision=lax.Precision.HIGHEST,
    )
    value_pool = jnp.einsum(
        "sp,skd->pkd",
        places,
        value_slots.reshape(slot_count, TILE, HD),
        precision=lax.Precision.HIGHEST,
    )
    return (grad_query.astype(jnp.bfloat16), key_pool, value_pool)


def per_device(query, keys, values, cotangent, kv_tiles):
    head_count = lax.axis_size("head")
    cycle_pos = lax.axis_index("blk")
    per_frame = query.shape[0] * head_count // TILE
    reach = -(-HALF // per_frame)
    span = (2 * reach + 1) * per_frame
    global_tiles = kv_tiles[:, 0, :GLOBALS]
    own_tiles = lax.dynamic_slice_in_dim(kv_tiles, cycle_pos * per_frame, per_frame, 1)
    moved = (
        lax.all_to_all(query, "head", split_axis=1, concat_axis=0, tiled=True),
        lax.all_to_all(keys, "head", split_axis=1, concat_axis=0, tiled=True),
        lax.all_to_all(values, "head", split_axis=1, concat_axis=0, tiled=True),
        lax.all_to_all(cotangent, "head", split_axis=1, concat_axis=0, tiled=True),
    )
    frame_keys = moved[1]
    frame_values = moved[2]
    offset = 1
    earlier = passed_along((frame_keys, frame_values), "blk", offset)
    later = passed_along((frame_keys, frame_values), "blk", -offset)
    earlier_keys = [earlier[0]]
    earlier_values = [earlier[1]]
    later_keys = [later[0]]
    later_values = [later[1]]
    near_keys = jnp.stack(earlier_keys[::-1] + later_keys, axis=0)
    near_values = jnp.stack(earlier_values[::-1] + later_values, axis=0)
    width = frame_keys.shape[1]
    all_keys = jnp.concatenate(
        [near_keys[:reach], frame_keys[None], near_keys[reach:]], axis=0
    ).reshape(span * TILE, width)
    all_values = jnp.concatenate(
        [near_values[:reach], frame_values[None], near_values[reach:]], axis=0
    ).reshape(span * TILE, width)
    own_keys = split_heads(frame_keys, per_frame)
    own_values = split_heads(frame_values, per_frame)
    tile_ids = cycle_pos * per_frame + jnp.arange(per_frame, dtype=jnp.int32)
    owner = global_tiles[:, :, None] == tile_ids[None, None, :]
    owner_mask = owner.astype(jnp.bfloat16)
    global_keys = jnp.einsum(
        "hjt,htkd->hjkd", owner_mask, own_keys, preferred_element_type=jnp.float32
    )
    global_values = jnp.einsum(
        "hjt,htkd->hjkd", owner_mask, own_values, preferred_element_type=jnp.float32
    )
    global_keys, global_values = (
        lax.psum(global_keys.astype(jnp.bfloat16), "blk").astype(jnp.float32),
        lax.psum(global_values.astype(jnp.bfloat16), "blk").astype(jnp.float32),
    )
    pool_keys = jnp.concatenate(
        [split_heads(all_keys, span), global_keys.astype(jnp.bfloat16)], axis=1
    )
    pool_values = jnp.concatenate(
        [split_heads(all_values, span), global_values.astype(jnp.bfloat16)], axis=1
    )
    relative = own_tiles - (cycle_pos - reach) * per_frame
    inside = (relative >= 0) & (relative < span)
    matches = own_tiles[:, :, :, None] == global_tiles[:, None, None, :]
    slot_numbers = jnp.arange(global_tiles.shape[1], dtype=jnp.int32)
    global_slot = jnp.sum(jnp.where(matches, slot_numbers[None, None, None, :], 0), axis=-1)
    pool_index = jnp.where(inside, relative, span + global_slot)
    queries = split_heads(moved[0], per_frame)
    grad_out = split_heads(moved[3], per_frame)
    attended, log_total = lax.map(attend_forward, (queries, pool_keys, pool_values, pool_index))
    grad_query, key_pool, value_pool = lax.map(
        attend_backward,
        (queries, pool_keys, pool_values, grad_out, attended, log_total, pool_index),
    )
    centre = reach * per_frame
    key_grad = key_pool[:, centre : centre + per_frame]
    value_grad = value_pool[:, centre : centre + per_frame]
    offset = 1
    lower = (reach - offset) * per_frame
    returned = (
        passed_along(
            key_pool[:, lower : lower + per_frame].astype(jnp.bfloat16), "blk", -offset
        ).astype(jnp.float32),
        passed_along(
            value_pool[:, lower : lower + per_frame].astype(jnp.bfloat16), "blk", -offset
        ).astype(jnp.float32),
    )
    key_grad = key_grad + returned[0]
    value_grad = value_grad + returned[1]
    upper = (reach + offset) * per_frame
    returned = (
        passed_along(
            key_pool[:, upper : upper + per_frame].astype(jnp.bfloat16), "blk", offset
        ).astype(jnp.float32),
        passed_along(
            value_pool[:, upper : upper + per_frame].astype(jnp.bfloat16), "blk", offset
        ).astype(jnp.float32),
    )
    key_grad = key_grad + returned[0]
    value_grad = value_grad + returned[1]
    summed = (
        lax.psum(key_pool[:, span:].astype(jnp.bfloat16), "blk").astype(jnp.float32),
        lax.psum(value_pool[:, span:].astype(jnp.bfloat16), "blk").astype(jnp.float32),
    )
    owner_float = owner.astype(jnp.float32)
    key_grad = key_grad + jnp.einsum(
        "hjt,hjkd->htkd", owner_float, summed[0], precision=lax.Precision.HIGHEST
    )
    value_grad = value_grad + jnp.einsum(
        "hjt,hjkd->htkd", owner_float, summed[1], precision=lax.Precision.HIGHEST
    )
    query_rows = merge_heads(grad_query)
    key_rows = merge_heads(key_grad.astype(jnp.bfloat16))
    value_rows = merge_heads(value_grad.astype(jnp.bfloat16))
    results = (
        lax.all_to_all(merge_heads(attended), "head", split_axis=0, concat_axis=1, tiled=True),
        lax.all_to_all(query_rows, "head", split_axis=0, concat_axis=1, tiled=True),
        lax.all_to_all(key_rows, "head", split_axis=0, concat_axis=1, tiled=True),
        lax.all_to_all(value_rows, "head", split_axis=0, concat_axis=1, tiled=True),
    )
    return (results[0], results[1], results[2], results[3])


def solution(mesh):
    placed = (
        P(("blk", "head"), None),
        P(("blk", "head"), None),
        P(("blk", "head"), None),
        P(("blk", "head"), None),
        P("head", None, None),
    )
    return jax.shard_map(
        per_device,
        mesh=mesh,
        in_specs=placed,
        out_specs=(
            P(("blk", "head"), None),
            P(("blk", "head"), None),
            P(("blk", "head"), None),
            P(("blk", "head"), None),
        ),
        check_vma=False,
    )
```

profile of v0, /device:TPU:160, one launch (start us, length us, event | category | flops | bytes accessed | tf_op | source)
XLA Modules:
  0.0 897.8 jit_solution(17046188124416074661)
XLA Ops:
  9.5 5.9 all-to-all-start.1
  16.6 10.3 %all-to-all-done.1 = bf16[128,8,384]{0,2,1:T(8,128)(2,1)S(1)} async-done(((bf16[128,8,384]{0,2,1:T(8,128)(2,1)}), bf16[128,8,384]{0,2,1:T(8,128)(2,1)S(1)}, u32[]{:S(2)}, u32[]{:S(2)}) %all-to-all-start.1) | async-done | bytes 786464 | tf_op jit(solution)/shard_map/all_to_all | solution.py:108
  26.9 4.2 all-to-all-start.2
  32.2 10.5 %all-to-all-done.2 = bf16[128,8,384]{0,2,1:T(8,128)(2,1)S(1)} async-done(((bf16[128,8,384]{0,2,1:T(8,128)(2,1)}), bf16[128,8,384]{0,2,1:T(8,128)(2,1)S(1)}, u32[]{:S(2)}, u32[]{:S(2)}) %all-to-all-start.2) | async-done | bytes 786464 | tf_op jit(solution)/shard_map/all_to_all | solution.py:109
  42.7 4.2 all-to-all-start
  47.4 4.0 collective-permute-start.3
  61.8 7.8 collective-permute-start.1
  72.8 6.1 all-to-all-start.4
  80.1 262.5 %all-reduce.7.cloned.1.call-done = (bf16[3,2,128,128]{3,1,2,0:T(2,128)(2,1)}, bf16[3,2,128,128]{3,1,2,0:T(2,128)(2,1)}) async-done(((bf16[3,2,128,128]{3,1,2,0:T(2,128)(2,1)}, bf16[3,2,128,128]{3,1,2,0:T(2,128)(2,1)}), (bf16[3,2,128,128]{3,1,2,0:T(2,128)(2,1)}, bf16[3,2,128,128]{3,1,2,0:T(2,128)(2,1)})) %all-reduce.7.cloned.1.call-update) | async-done | bytes 393232 | tf_op jit(solution)/shard_map/psum | solution.py:142
  348.6 5.9 reshape_reshape.7
  363.1 5.9 reshape_reshape.6
  373.4 32.2 %while.26 = (s32[]{:T(128)}, bf16[3,8,128,128]{3,2,1,0:T(8,128)(2,1)}, f32[3,8,128,1,1]{2,1,4,3,0:T(8,128)S(1)}, bf16[3,8,128,128]{3,2,1,0:T(8,128)(2,1)}, bf16[...) while((s32[]{:T(128)}, ...), condition=%wide.region_6.8_spmd, body=%wide.region_3.7_spmd.sunk | while | flops 615907776 | bytes 41720132 | solution.py:159
  407.9 5.7 all-to-all-start.3
  413.6 115.5 %while.27 = (s32[]{:T(128)}, bf16[3,8,128,128]{2,3,0,1:T(8,128)(2,1)}, f32[3,26,128,128]{3,1,2,0:T(8,128)}, f32[3,26,128,128]{3,1,2,0:T(8,128)}, bf16[3,8,128,12...) while((s32[]{:T(128)}, ...), condition=%wide.region_9.11_spmd, body=%wide.region_7.10_spmd.sunk | while | flops 2260996352 | bytes 105939144 | solution.py:160
  438.7 3.4 fusion.140
  443.1 8.2 bitcast_dynamic-update-slice_fusion.8
  453.2 6.0 bitcast_dynamic-update-slice_fusion.7
  473.7 3.4 fusion.140
  478.0 8.2 bitcast_dynamic-update-slice_fusion.8
  488.1 6.0 bitcast_dynamic-update-slice_fusion.7
  512.9 8.2 bitcast_dynamic-update-slice_fusion.8
  523.0 6.0 bitcast_dynamic-update-slice_fusion.7
  529.0 3.5 convert.12
  532.6 5.7 all-to-all-start.5
  545.8 3.6 convert.11
  550.2 279.6 %all-reduce.5.cloned.1.call-done = (bf16[3,2,128,128]{3,1,2,0:T(2,128)(2,1)}, bf16[3,2,128,128]{3,1,2,0:T(2,128)(2,1)}) async-done(((bf16[3,2,128,128]{3,1,2,0:T(2,128)(2,1)}, bf16[3,2,128,128]{3,1,2,0:T(2,128)(2,1)}), (bf16[3,2,128,128]{3,1,2,0:T(2,128)(2,1)}, bf16[3,2,128,128]{3,1,2,0:T(2,128)(2,1)})) %all-reduce.5.cloned.1.call-update) | async-done | bytes 393232 | tf_op jit(solution)/shard_map/psum | solution.py:191
  829.8 3.5 fusion.74
  835.7 5.8 all-to-all-start.7
  841.8 3.9 collective-permute-start.4
  847.7 13.1 %collective-permute-done.4 = bf16[3,8,128,128]{3,1,2,0:T(8,128)(2,1)S(1)} collective-permute-done((bf16[3,8,128,128]{3,1,2,0:T(8,128)(2,1)S(1)}, bf16[3,8,128,128]{3,1,2,0:T(8,128)(2,1)S(1)}, u32[]{:S(2)}, u32[]{:S(2)}) %collective-permute-start.4) | collective-permute-done | bytes 786464 | tf_op jit(solution)/shard_map/ppermute | solution.py:15
  860.8 11.0 %collective-permute-done.5 = bf16[3,8,128,128]{3,1,2,0:T(8,128)(2,1)S(1)} collective-permute-done((bf16[3,8,128,128]{3,1,2,0:T(8,128)(2,1)S(1)}, bf16[3,8,128,128]{3,1,2,0:T(8,128)(2,1)S(1)}, u32[]{:S(2)}, u32[]{:S(2)}) %collective-permute-start.5) | collective-permute-done | bytes 786464 | tf_op jit(solution)/shard_map/ppermute | solution.py:15
  875.2 5.7 all-to-all-start.6
  (197 shorter events, 154.4 us)
Async XLA Ops:
  7.2 8.3 copy-start.5
  9.5 21.5 %copy-start.6 = (bf16[128,3072]{1,0:T(8,128)(2,1)S(1)}, bf16[128,3072]{1,0:T(8,128)(2,1)}, u32[]{:S(2)}) copy-start(bf16[128,3072]{1,0:T(8,128)(2,1)} %param.11) | copy-start | bytes 2359300
  9.5 17.3 %all-to-all-start.1 = ((bf16[128,8,384]{0,2,1:T(8,128)(2,1)}), bf16[128,8,384]{0,2,1:T(8,128)(2,1)S(1)}, u32[]{:S(2)}, u32[]{:S(2)}) async-start(bf16[128,8,384]{0,2,1:T(8,128)(2,1)} %bitcast.39), calls=%async_computation.1 | async-start | bytes 1572864 | tf_op jit(solution)/shard_map/all_to_all | solution.py:108
  16.6 30.3 %copy-start.11 = (s32[3,256,9]{1,0,2:T(4,128)S(1)}, s32[3,256,9]{1,0,2:T(4,128)}, u32[]{:S(2)}) copy-start(s32[3,256,9]{1,0,2:T(4,128)} %param.15) | copy-start | bytes 82948
  26.9 15.8 %all-to-all-start.2 = ((bf16[128,8,384]{0,2,1:T(8,128)(2,1)}), bf16[128,8,384]{0,2,1:T(8,128)(2,1)S(1)}, u32[]{:S(2)}, u32[]{:S(2)}) async-start(bf16[128,8,384]{0,2,1:T(8,128)(2,1)} %bitcast.50), calls=%async_computation.2 | async-start | bytes 1572864 | tf_op jit(solution)/shard_map/all_to_all | solution.py:109
  42.7 30.2 %all-to-all-start = ((bf16[128,8,384]{0,2,1:T(8,128)(2,1)}), bf16[128,8,384]{0,2,1:T(8,128)(2,1)S(1)}, u32[]{:S(2)}, u32[]{:S(2)}) async-start(bf16[128,8,384]{0,2,1:T(8,128)(2,1)} %bitcast.35), calls=%async_computation | async-start | bytes 1572864 | tf_op jit(solution)/shard_map/all_to_all | solution.py:107
  46.9 295.8 %all-reduce.7.cloned.1.call-start = ((), (), s32[]{:S(2)}) async-start(), calls=%async_computation.9 | async-start | bytes 786432 | tf_op jit(solution)/shard_map/psum | solution.py:142
  47.0 13.6 %copy-start.9 = (s32[3,1,2]{2,0,1:T(4,128)}, s32[3,1,2]{2,0,1:T(4,128)S(1)}, u32[]{:S(2)}) copy-start(s32[3,1,2]{2,0,1:T(4,128)S(1)} %copy.129) | copy-start | bytes 76
  47.0 11.1 %copy-start.12 = (s32[8]{0:T(128)}, s32[8]{0:T(128)S(1)}, u32[]{:S(2)}) copy-start(s32[8]{0:T(128)S(1)} %iota_add_fusion) | copy-start | bytes 100
  47.4 298.2 %collective-permute-start.3 = (bf16[1024,384]{1,0:T(8,128)(2,1)S(1)}, bf16[1024,384]{1,0:T(8,128)(2,1)}, u32[]{:S(2)}, u32[]{:S(2)}) collective-permute-start(bf16[1024,384]{1,0:T(8,128)(2,1)S(1)} %bitcast.238), channel_id=1, source_target_pairs={{8,0},{16,8},{24,16},{32,24},{40,32},{48,40},{56,48},{64,56},{72,6... | collective-permute-start | bytes 2359304 | tf_op jit(solution)/shard_map/ppermute | solution.py:15
  51.3 294.2 %collective-permute-start.2 = (bf16[1024,384]{1,0:T(8,128)(2,1)S(1)}, bf16[1024,384]{1,0:T(8,128)(2,1)}, u32[]{:S(2)}, u32[]{:S(2)}) collective-permute-start(bf16[1024,384]{1,0:T(8,128)(2,1)S(1)} %bitcast.239), channel_id=1, source_target_pairs={{0,8},{8,16},{16,24},{24,32},{32,40},{40,48},{48,56},{56,64},{64,7... | collective-permute-start | bytes 2359304 | tf_op jit(solution)/shard_map/ppermute | solution.py:15
  58.1 13.6 %copy-start.7 = (bf16[128,3072]{1,0:T(8,128)(2,1)S(1)}, bf16[128,3072]{1,0:T(8,128)(2,1)}, u32[]{:S(2)}) copy-start(bf16[128,3072]{1,0:T(8,128)(2,1)} %param.14) | copy-start | bytes 2359300
  61.8 298.0 %collective-permute-start.1 = (bf16[1024,384]{1,0:T(8,128)(2,1)}, bf16[1024,384]{1,0:T(8,128)(2,1)}, u32[]{:S(2)}, u32[]{:S(2)}) collective-permute-start(bf16[1024,384]{1,0:T(8,128)(2,1)} %bitcast.41), channel_id=1, source_target_pairs={{8,0},{16,8},{24,16},{32,24},{40,32},{48,40},{56,48},{64,56},{72,6... | collective-permute-start | bytes 2359304 | tf_op jit(solution)/shard_map/ppermute | solution.py:15
  69.7 290.2 %collective-permute-start = (bf16[1024,384]{1,0:T(8,128)(2,1)}, bf16[1024,384]{1,0:T(8,128)(2,1)}, u32[]{:S(2)}, u32[]{:S(2)}) collective-permute-start(bf16[1024,384]{1,0:T(8,128)(2,1)} %bitcast.41), channel_id=1, source_target_pairs={{0,8},{8,16},{16,24},{24,32},{32,40},{40,48},{48,56},{56,64},{64,7... | collective-permute-start | bytes 2359304 | tf_op jit(solution)/shard_map/ppermute | solution.py:15
  72.8 335.0 %all-to-all-start.4 = ((bf16[128,8,384]{0,2,1:T(8,128)(2,1)}), bf16[128,8,384]{0,2,1:T(8,128)(2,1)}, u32[]{:S(2)}, u32[]{:S(2)}) async-start(bf16[128,8,384]{0,2,1:T(8,128)(2,1)} %bitcast.66), calls=%async_computation.4 | async-start | bytes 1572864 | tf_op jit(solution)/shard_map/all_to_all | solution.py:110
  407.9 124.7 %all-to-all-start.3 = ((bf16[8,128,384]{1,2,0:T(8,128)(2,1)}), bf16[8,128,384]{1,2,0:T(8,128)(2,1)}, u32[]{:S(2)}, u32[]{:S(2)}) async-start(bf16[8,128,384]{1,2,0:T(8,128)(2,1)} %bitcast.61), calls=%async_computation.3 | async-start | bytes 1572864 | tf_op jit(solution)/shard_map/all_to_all | solution.py:205
  430.7 2.4 copy-start
  443.1 8.2 copy-start.4
  465.6 2.4 copy-start
  478.0 8.2 copy-start.4
  512.9 8.2 copy-start.4
  532.6 303.1 %all-to-all-start.5 = ((bf16[8,128,384]{1,2,0:T(8,128)(2,1)}), bf16[8,128,384]{1,2,0:T(8,128)(2,1)}, u32[]{:S(2)}, u32[]{:S(2)}) async-start(bf16[8,128,384]{1,2,0:T(8,128)(2,1)} %bitcast.244), calls=%async_computation.5 | async-start | bytes 1572864 | tf_op jit(solution)/shard_map/all_to_all | solution.py:206
  538.3 291.5 %all-reduce.5.cloned.1.call-start = ((), (), s32[]{:S(2)}) async-start(), calls=%async_computation.8 | async-start | bytes 786432 | tf_op jit(solution)/shard_map/psum | solution.py:191
  539.7 290.1 %collective-permute-start.6 = (bf16[3,8,128,128]{3,1,2,0:T(8,128)(2,1)}, bf16[3,8,128,128]{3,1,2,0:T(8,128)(2,1)}, u32[]{:S(2)}, u32[]{:S(2)}) collective-permute-start(bf16[3,8,128,128]{3,1,2,0:T(8,128)(2,1)} %get-tuple-element.225), channel_id=1, source_target_pairs={{8,0},{16,8},{24,16},{32,24},{40,32},{48,40},{56,48},{64,56},{72,6... | collective-permute-start | bytes 2359304 | tf_op jit(solution)/shard_map/ppermute | solution.py:15
  543.1 286.7 %collective-permute-start.7 = (bf16[3,8,128,128]{3,1,2,0:T(8,128)(2,1)}, bf16[3,8,128,128]{3,1,2,0:T(8,128)(2,1)}, u32[]{:S(2)}, u32[]{:S(2)}) collective-permute-start(bf16[3,8,128,128]{3,1,2,0:T(8,128)(2,1)} %get-tuple-element.226), channel_id=1, source_target_pairs={{0,8},{8,16},{16,24},{24,32},{32,40},{40,48},{48,56},{56,64},{64,7... | collective-permute-start | bytes 2359304 | tf_op jit(solution)/shard_map/ppermute | solution.py:15
  545.8 284.0 %copy-start.10 = (s32[3,1,2]{2,0,1:T(4,128)S(1)}, s32[3,1,2]{2,0,1:T(4,128)}, u32[]{:S(2)}) copy-start(s32[3,1,2]{2,0,1:T(4,128)} %copy-done.9) | copy-start | bytes 76
  545.8 284.0 %copy-start.13 = (s32[8]{0:T(128)S(1)}, s32[8]{0:T(128)}, u32[]{:S(2)}) copy-start(s32[8]{0:T(128)} %copy-done.12) | copy-start | bytes 100
  835.7 36.1 %copy-start.8 = (bf16[3,2,128,128]{3,1,2,0:T(2,128)(2,1)S(1)}, bf16[3,2,128,128]{3,1,2,0:T(2,128)(2,1)}, u32[]{:S(2)}) copy-start(bf16[3,2,128,128]{3,1,2,0:T(2,128)(2,1)} %get-tuple-element.209) | copy-start | bytes 589828
  835.7 39.6 %all-to-all-start.7 = ((bf16[8,128,384]{1,2,0:T(8,128)(2,1)}), bf16[8,128,384]{1,2,0:T(8,128)(2,1)}, u32[]{:S(2)}, u32[]{:S(2)}) async-start(bf16[8,128,384]{1,2,0:T(8,128)(2,1)} %bitcast.242), calls=%async_computation.7 | async-start | bytes 1572864 | tf_op jit(solution)/shard_map/all_to_all | solution.py:208
  841.8 19.0 %collective-permute-start.4 = (bf16[3,8,128,128]{3,1,2,0:T(8,128)(2,1)S(1)}, bf16[3,8,128,128]{3,1,2,0:T(8,128)(2,1)S(1)}, u32[]{:S(2)}, u32[]{:S(2)}) collective-permute-start(bf16[3,8,128,128]{3,1,2,0:T(8,128)(2,1)S(1)} %get-tuple-element.227), channel_id=1, source_target_pairs={{8,0},{16,8},{24,16},{32,24},{40,32},{48,40},{56,48},{64,56},{72,6... | collective-permute-start | bytes 2359304 | tf_op jit(solution)/shard_map/ppermute | solution.py:15
  845.7 26.1 %collective-permute-start.5 = (bf16[3,8,128,128]{3,1,2,0:T(8,128)(2,1)S(1)}, bf16[3,8,128,128]{3,1,2,0:T(8,128)(2,1)S(1)}, u32[]{:S(2)}, u32[]{:S(2)}) collective-permute-start(bf16[3,8,128,128]{3,1,2,0:T(8,128)(2,1)S(1)} %get-tuple-element.228), channel_id=1, source_target_pairs={{0,8},{8,16},{16,24},{24,32},{32,40},{40,48},{48,56},{56,64},{64,7... | collective-permute-start | bytes 2359304 | tf_op jit(solution)/shard_map/ppermute | solution.py:15
  875.2 14.3 %all-to-all-start.6 = ((bf16[8,128,384]{1,2,0:T(8,128)(2,1)}), bf16[8,128,384]{1,2,0:T(8,128)(2,1)S(1)}, u32[]{:S(2)}, u32[]{:S(2)}) async-start(bf16[8,128,384]{1,2,0:T(8,128)(2,1)} %bitcast.75), calls=%async_computation.6 | async-start | bytes 1572864 | tf_op jit(solution)/shard_map/all_to_all | solution.py:207
  (10 other events, 17.9 us)
Sparse Core Ops, SparseCore 0:
  60.5 282.0 all-reduce.6
  550.3 279.4 all-reduce.4
where the time goes:
time: 904 us; the launch traced here: 898 us
  waiting for transfers between devices  589 us (65%)
  matrix products  95.7 us (11%)
  local copies, waits for them, and re-layouts  92.7 us (10%)
  starting transfers between devices  70.2 us (8%)
  other arithmetic  24.9 us (3%)
  between operations  14.5 us (2%)
  loops' own time  11 us (1%)
    psum x1, waiting for transfers between devices, per_device(): lax.psum(key_pool[:, span:].astype(jnp.bfloat16), 'blk').astype(jnp.float32)  280 us
    psum x1, waiting for transfers between devices, per_device(): lax.psum(global_keys.astype(jnp.bfloat16), 'blk').astype(jnp.float32)  262 us
    ppermute x8, starting transfers between devices, passed_along(): return lax.ppermute(block, axis, route)  26.8 us
    dot_general x3, matrix products, attend_backward(): jnp.einsum('sp,skd->pkd', places, value_slots.reshape(slot_count, TILE, H...  24.7 us
    ppermute x8, waiting for transfers between devices, passed_along(): return lax.ppermute(block, axis, route)  24.1 us
  transfers between devices with their start and end apart: 18, of which 7 were waited for; matrix products, arithmetic and copies ran while one was open for 23% of the time, Pallas kernels for 0%

commit v1 on v0

--- a/solution.py
+++ b/solution.py
@@ -13,6 +13,18 @@
     devices = range(lax.axis_size(axis))
     route = [(i - distance, i) for i in devices if i - distance in devices]
     return lax.ppermute(block, axis, route)
+
+
+def butterfly_sum(block, axis):
+    count = lax.axis_size(axis)
+    if count & (count - 1):
+        return lax.psum(block, axis)
+    stride = 1
+    while stride < count:
+        route = [(i, i ^ stride) for i in range(count)]
+        block = block + lax.ppermute(block, axis, route)
+        stride *= 2
+    return block
 
 
 def split_heads(field, count):
@@ -138,10 +150,10 @@
     global_values = jnp.einsum(
         "hjt,htkd->hjkd", owner_mask, own_values, preferred_element_type=jnp.float32
     )
-    global_keys, global_values = (
-        lax.psum(global_keys.astype(jnp.bfloat16), "blk").astype(jnp.float32),
-        lax.psum(global_values.astype(jnp.bfloat16), "blk").astype(jnp.float32),
-    )
+    global_both = butterfly_sum(
+        jnp.stack([global_keys.astype(jnp.bfloat16), global_values.astype(jnp.bfloat16)]), "blk"
+    ).astype(jnp.float32)
+    global_keys, global_values = global_both[0], global_both[1]
     pool_keys = jnp.concatenate(
         [split_heads(all_keys, span), global_keys.astype(jnp.bfloat16)], axis=1
     )
@@ -187,10 +199,7 @@
     )
     key_grad = key_grad + returned[0]
     value_grad = value_grad + returned[1]
-    summed = (
-        lax.psum(key_pool[:, span:].astype(jnp.bfloat16), "blk").astype(jnp.float32),
-        lax.psum(value_pool[:, span:].astype(jnp.bfloat16), "blk").astype(jnp.float32),
-    )
+    summed = butterfly_sum(jnp.stack([key_pool[:, span:], value_pool[:, span:]]), "blk")
     owner_float = owner.astype(jnp.float32)
     key_grad = key_grad + jnp.einsum(
         "hjt,hjkd->htkd", owner_float, summed[0], precision=lax.Precision.HIGHEST

time: 904 us -> 526 us (0.58)
  waiting for transfers between devices: 589 us -> 159 us
  starting transfers between devices: 70.2 us -> 122 us
  between operations: 14.5 us -> 1.45 us
  other arithmetic: 24.9 us -> 36.2 us
    psum x2 -> x0, waiting for transfers between devices: 542 us -> none  [the longest x1 280 us: per_device(): lax.psum(key_pool[:, span:].astype(jnp.bfloat16), 'blk').astype(jnp.float32)]
    ppermute x0 -> x10, waiting for transfers between devices: none -> 87.3 us  [butterfly_sum(): block = block + lax.ppermute(block, axis, route)]
    all_to_all x1, starting transfers between devices: 6.14 us -> 39.9 us  [per_device(): lax.all_to_all(cotangent, 'head', split_axis=1, concat_axis=0, tiled=True)]
    ppermute x8, waiting for transfers between devices: 24.1 us -> 49.2 us  [passed_along(): return lax.ppermute(block, axis, route)]
    ppermute x0 -> x10, starting transfers between devices: none -> 18.2 us  [butterfly_sum(): block = block + lax.ppermute(block, axis, route)]
    add x0 -> x10, other arithmetic: none -> 11.2 us  [butterfly_sum(): block = block + lax.ppermute(block, axis, route)]
  transfers between devices with their start and end apart: 18 -> 26, of which waited for: 7 -> 16; matrix products, arithmetic and copies ran while one was open for 23% -> 20% of each run, Pallas kernels for 0% -> 0%
where the time goes in v1:
time: 526 us; the launch traced here: 516 us
  waiting for transfers between devices  159 us (30%)
  starting transfers between devices  122 us (23%)
  matrix products  93 us (18%)
  local copies, waits for them, and re-layouts  92.6 us (18%)
  other arithmetic  36.2 us (7%)
  loops' own time  11.3 us (2%)
    ppermute x10, waiting for transfers between devices, butterfly_sum(): block = block + lax.ppermute(block, axis, route)  87.3 us
    ppermute x8, waiting for transfers between devices, passed_along(): return lax.ppermute(block, axis, route)  49.2 us
    all_to_all x1, starting transfers between devices, per_device(): lax.all_to_all(cotangent, 'head', split_axis=1, concat_axis=0, tiled=True)  39.9 us
    ppermute x8, starting transfers between devices, passed_along(): return lax.ppermute(block, axis, route)  24.8 us
    dot_general x3, matrix products, attend_backward(): jnp.einsum('sp,skd->pkd', places, value_slots.reshape(slot_count, TILE, H...  24.6 us
    ppermute x10, starting transfers between devices, butterfly_sum(): block = block + lax.ppermute(block, axis, route)  18.2 us
    dot_general x3, matrix products, attend_backward(): jnp.einsum('sp,skd->pkd', places, key_slots.reshape(slot_count, TILE, HD)...  17.9 us
    unnamed x29, local copies, waits for them, and re-layouts  16.4 us
  transfers between devices with their start and end apart: 26, of which 16 were waited for; matrix products, arithmetic and copies ran while one was open for 20% of the time, Pallas kernels for 0%

profile of v1, /device:TPU:160, one launch (start us, length us, event | category | flops | bytes accessed | tf_op | source)
XLA Modules:
  0.0 515.9 jit_solution(13771178838250289576)
XLA Ops:
  3.0 5.8 %all-to-all-start.1 = ((bf16[128,8,384]{0,2,1:T(8,128)(2,1)}), bf16[128,8,384]{0,2,1:T(8,128)(2,1)S(1)}, u32[]{:S(2)}, u32[]{:S(2)}) async-start(bf16[128,8,384]{0,2,1:T(8,128)(2,1)} %bitcast.39), calls=%async_computation.1 | async-start | bytes 1572864 | tf_op jit(solution)/shard_map/all_to_all | solution.py:120
  9.9 10.3 %all-to-all-done.1 = bf16[128,8,384]{0,2,1:T(8,128)(2,1)S(1)} async-done(((bf16[128,8,384]{0,2,1:T(8,128)(2,1)}), bf16[128,8,384]{0,2,1:T(8,128)(2,1)S(1)}, u32[]{:S(2)}, u32[]{:S(2)}) %all-to-all-start.1) | async-done | bytes 786464 | tf_op jit(solution)/shard_map/all_to_all | solution.py:120
  20.2 4.2 all-to-all-start.2
  25.6 10.4 %all-to-all-done.2 = bf16[128,8,384]{0,2,1:T(8,128)(2,1)S(1)} async-done(((bf16[128,8,384]{0,2,1:T(8,128)(2,1)}), bf16[128,8,384]{0,2,1:T(8,128)(2,1)S(1)}, u32[]{:S(2)}, u32[]{:S(2)}) %all-to-all-start.2) | async-done | bytes 786464 | tf_op jit(solution)/shard_map/all_to_all | solution.py:121
  44.3 4.2 all-to-all-start
  61.5 5.0 collective-permute-done.4
  75.9 8.0 %collective-permute-done.5 = bf16[2,3,2,128,128]{4,2,3,1,0:T(2,128)(2,1)S(1)} collective-permute-done((bf16[2,3,2,128,128]{4,2,3,1,0:T(2,128)(2,1)S(1)}, bf16[2,3,2,128,128]{4,2,3,1,0:T(2,128)(2,1)S(1)}, u32[]{:S(2)}, u32[]{:S(2)}) %collective-permute-start.5) | collective-permute-done | bytes 393248 | tf_op jit(solution)/shard_map/ppermute | solution.py:25
  89.6 39.9 %all-to-all-start.4 = ((bf16[128,8,384]{0,2,1:T(8,128)(2,1)}), bf16[128,8,384]{0,2,1:T(8,128)(2,1)}, u32[]{:S(2)}, u32[]{:S(2)}) async-start(bf16[128,8,384]{0,2,1:T(8,128)(2,1)} %bitcast.70), calls=%async_computation.4 | async-start | bytes 1572864 | tf_op jit(solution)/shard_map/all_to_all | solution.py:122
  133.8 5.9 %reshape_reshape.7 = bf16[24,128,3,128]{3,2,1,0:T(4,128)(2,1)S(1)} reshape(bf16[3,1024,384]{2,1,0:T(8,128)(2,1)} %pad_maximum_fusion.3) | data formatting | bytes 4718592 | tf_op jit(solution)/shard_map/reshape;reshape | solution.py:32
  143.1 7.0 %reshape_reshape.6 = bf16[24,128,3,128]{3,2,1,0:T(4,128)(2,1)} reshape(bf16[3,1024,384]{2,1,0:T(8,128)(2,1)} %pad_maximum_fusion.2) | data formatting | bytes 4718592 | tf_op jit(solution)/shard_map/reshape;reshape | solution.py:32
  161.2 32.5 %while.26 = (s32[]{:T(128)}, bf16[3,8,128,128]{3,2,1,0:T(8,128)(2,1)}, f32[3,8,128,1,1]{2,1,4,3,0:T(8,128)S(1)}, bf16[3,8,128,128]{3,2,1,0:T(8,128)(2,1)}, bf16[...) while((s32[]{:T(128)}, ...), condition=%wide.region_4.6_spmd, body=%wide.region_1.5_spmd.sunk | while | flops 615907776 | bytes 41720132 | solution.py:171
  193.6 116.0 %while.27 = (s32[]{:T(128)}, bf16[3,8,128,128]{2,3,0,1:T(8,128)(2,1)}, f32[3,26,128,128]{3,1,2,0:T(8,128)}, f32[3,26,128,128]{3,1,2,0:T(8,128)}, bf16[3,8,128,12...) while((s32[]{:T(128)}, ...), condition=%wide.region_7.9_spmd, body=%wide.region_5.8_spmd.sunk | while | flops 2260996352 | bytes 105939144 | solution.py:172
  223.4 8.2 %bitcast_dynamic-update-slice_fusion.8 = f32[3,26,128,128]{3,1,2,0:T(8,128)} fusion(f32[3,26,128,128]{3,1,2,0:T(8,128)} %get-tuple-element.402, s32[]{:T(128)S(6)} %copy.170, f32[72,128,128]{2,1,0:T(8,128)} %bitcast.241, s32[72]{0:T(128)S(1)} %eq.132), kind=kOutput, calls=%fused_computation.49.clone.1 | convolution fusion | flops 368052032 | bytes 6816036 | tf_op jit(solution)/shard_map/while/body/eval_jaxpr/sp,skd->pkd/dot_general | solution.py:101
  233.5 6.0 %bitcast_dynamic-update-slice_fusion.7 = f32[3,26,128,128]{3,1,2,0:T(8,128)} fusion(f32[3,26,128,128]{3,1,2,0:T(8,128)} %get-tuple-element.401, s32[]{:T(128)S(6)} %copy.170, f32[72,128,128]{2,1,0:T(8,128)S(1)} %bitcast.242, s32[72]{0:T(128)S(1)} %eq.132), kind=kOutput, calls=%fused_computation.50.clone.1 | convolution fusion | flops 368052032 | bytes 6816036 | tf_op jit(solution)/shard_map/while/body/eval_jaxpr/sp,skd->pkd/dot_general | solution.py:95
  258.4 8.2 %bitcast_dynamic-update-slice_fusion.8 = f32[3,26,128,128]{3,1,2,0:T(8,128)} fusion(f32[3,26,128,128]{3,1,2,0:T(8,128)} %get-tuple-element.402, s32[]{:T(128)S(6)} %copy.170, f32[72,128,128]{2,1,0:T(8,128)} %bitcast.241, s32[72]{0:T(128)S(1)} %eq.132), kind=kOutput, calls=%fused_computation.49.clone.1 | convolution fusion | flops 368052032 | bytes 6816036 | tf_op jit(solution)/shard_map/while/body/eval_jaxpr/sp,skd->pkd/dot_general | solution.py:101
  268.4 6.0 %bitcast_dynamic-update-slice_fusion.7 = f32[3,26,128,128]{3,1,2,0:T(8,128)} fusion(f32[3,26,128,128]{3,1,2,0:T(8,128)} %get-tuple-element.401, s32[]{:T(128)S(6)} %copy.170, f32[72,128,128]{2,1,0:T(8,128)S(1)} %bitcast.242, s32[72]{0:T(128)S(1)} %eq.132), kind=kOutput, calls=%fused_computation.50.clone.1 | convolution fusion | flops 368052032 | bytes 6816036 | tf_op jit(solution)/shard_map/while/body/eval_jaxpr/sp,skd->pkd/dot_general | solution.py:95
  293.4 8.2 %bitcast_dynamic-update-slice_fusion.8 = f32[3,26,128,128]{3,1,2,0:T(8,128)} fusion(f32[3,26,128,128]{3,1,2,0:T(8,128)} %get-tuple-element.402, s32[]{:T(128)S(6)} %copy.170, f32[72,128,128]{2,1,0:T(8,128)} %bitcast.241, s32[72]{0:T(128)S(1)} %eq.132), kind=kOutput, calls=%fused_computation.49.clone.1 | convolution fusion | flops 368052032 | bytes 6816036 | tf_op jit(solution)/shard_map/while/body/eval_jaxpr/sp,skd->pkd/dot_general | solution.py:101
  303.5 6.0 %bitcast_dynamic-update-slice_fusion.7 = f32[3,26,128,128]{3,1,2,0:T(8,128)} fusion(f32[3,26,128,128]{3,1,2,0:T(8,128)} %get-tuple-element.401, s32[]{:T(128)S(6)} %copy.170, f32[72,128,128]{2,1,0:T(8,128)S(1)} %bitcast.242, s32[72]{0:T(128)S(1)} %eq.132), kind=kOutput, calls=%fused_computation.50.clone.1 | convolution fusion | flops 368052032 | bytes 6816036 | tf_op jit(solution)/shard_map/while/body/eval_jaxpr/sp,skd->pkd/dot_general | solution.py:95
  317.2 5.7 %all-to-all-start.3 = ((bf16[8,128,384]{1,2,0:T(8,128)(2,1)}), bf16[8,128,384]{1,2,0:T(8,128)(2,1)}, u32[]{:S(2)}, u32[]{:S(2)}) async-start(bf16[8,128,384]{1,2,0:T(8,128)(2,1)} %bitcast.65), calls=%async_computation.3 | async-start | bytes 1572864 | tf_op jit(solution)/shard_map/all_to_all | solution.py:214
  322.9 12.9 %collective-permute-done.12 = f32[2,3,2,128,128]{4,2,3,1,0:T(2,128)S(1)} collective-permute-done((f32[2,3,2,128,128]{4,2,3,1,0:T(2,128)}, f32[2,3,2,128,128]{4,2,3,1,0:T(2,128)S(1)}, u32[]{:S(2)}, u32[]{:S(2)}) %collective-permute-start.12) | collective-permute-done | bytes 786464 | tf_op jit(solution)/shard_map/ppermute | solution.py:25
  339.9 17.6 %collective-permute-done.13 = f32[2,3,2,128,128]{4,2,3,1,0:T(2,128)S(1)} collective-permute-done((f32[2,3,2,128,128]{4,2,3,1,0:T(2,128)S(1)}, f32[2,3,2,128,128]{4,2,3,1,0:T(2,128)S(1)}, u32[]{:S(2)}, u32[]{:S(2)}) %collective-permute-start.13) | collective-permute-done | bytes 786464 | tf_op jit(solution)/shard_map/ppermute | solution.py:25
  365.8 5.1 all-to-all-start.5
  371.2 23.7 %collective-permute-done.14 = f32[2,3,2,128,128]{4,2,3,1,0:T(2,128)} collective-permute-done((f32[2,3,2,128,128]{4,2,3,1,0:T(2,128)}, f32[2,3,2,128,128]{4,2,3,1,0:T(2,128)}, u32[]{:S(2)}, u32[]{:S(2)}) %collective-permute-start.14) | collective-permute-done | bytes 786464 | tf_op jit(solution)/shard_map/ppermute | solution.py:25
  398.4 8.5 %collective-permute-start.16 = (bf16[3,8,128,128]{3,1,2,0:T(8,128)(2,1)S(1)}, bf16[3,8,128,128]{3,1,2,0:T(8,128)(2,1)S(1)}, u32[]{:S(2)}, u32[]{:S(2)}) collective-permute-start(bf16[3,8,128,128]{3,1,2,0:T(8,128)(2,1)S(1)} %get-tuple-element.221), channel_id=1, source_target_pairs={{8,0},{16,8},{24,16},{32,24},{40,32},{48,40},{56,48},{64,56},{72,6... | collective-permute-start | bytes 2359304 | tf_op jit(solution)/shard_map/ppermute | solution.py:15
  412.4 12.9 %collective-permute-done.15 = f32[2,3,2,128,128]{4,2,3,1,0:T(2,128)S(1)} collective-permute-done((f32[2,3,2,128,128]{4,2,3,1,0:T(2,128)S(1)}, f32[2,3,2,128,128]{4,2,3,1,0:T(2,128)S(1)}, u32[]{:S(2)}, u32[]{:S(2)}) %collective-permute-start.15) | collective-permute-done | bytes 786464 | tf_op jit(solution)/shard_map/ppermute | solution.py:25
  425.8 15.0 %collective-permute-done.16 = bf16[3,8,128,128]{3,1,2,0:T(8,128)(2,1)S(1)} collective-permute-done((bf16[3,8,128,128]{3,1,2,0:T(8,128)(2,1)S(1)}, bf16[3,8,128,128]{3,1,2,0:T(8,128)(2,1)S(1)}, u32[]{:S(2)}, u32[]{:S(2)}) %collective-permute-start.16) | collective-permute-done | bytes 786464 | tf_op jit(solution)/shard_map/ppermute | solution.py:15
  440.8 11.3 %collective-permute-done.17 = bf16[3,8,128,128]{3,1,2,0:T(8,128)(2,1)S(1)} collective-permute-done((bf16[3,8,128,128]{3,1,2,0:T(8,128)(2,1)S(1)}, bf16[3,8,128,128]{3,1,2,0:T(8,128)(2,1)S(1)}, u32[]{:S(2)}, u32[]{:S(2)}) %collective-permute-start.17) | collective-permute-done | bytes 786464 | tf_op jit(solution)/shard_map/ppermute | solution.py:15
  452.2 3.7 fusion.76
  458.2 6.9 %all-to-all-start.7 = ((bf16[8,128,384]{1,2,0:T(8,128)(2,1)}), bf16[8,128,384]{1,2,0:T(8,128)(2,1)}, u32[]{:S(2)}, u32[]{:S(2)}) async-start(bf16[8,128,384]{1,2,0:T(8,128)(2,1)} %bitcast.259), calls=%async_computation.7 | async-start | bytes 1572864 | tf_op jit(solution)/shard_map/all_to_all | solution.py:217
  471.2 9.1 %collective-permute-done.9 = bf16[3,8,128,128]{3,1,2,0:T(8,128)(2,1)S(1)} collective-permute-done((bf16[3,8,128,128]{3,1,2,0:T(8,128)(2,1)S(1)}, bf16[3,8,128,128]{3,1,2,0:T(8,128)(2,1)S(1)}, u32[]{:S(2)}, u32[]{:S(2)}) %collective-permute-start.9) | collective-permute-done | bytes 786464 | tf_op jit(solution)/shard_map/ppermute | solution.py:15
  480.3 13.7 %collective-permute-done.10 = bf16[3,8,128,128]{3,1,2,0:T(8,128)(2,1)S(1)} collective-permute-done((bf16[3,8,128,128]{3,1,2,0:T(8,128)(2,1)S(1)}, bf16[3,8,128,128]{3,1,2,0:T(8,128)(2,1)S(1)}, u32[]{:S(2)}, u32[]{:S(2)}) %collective-permute-start.10) | collective-permute-done | bytes 786464 | tf_op jit(solution)/shard_map/ppermute | solution.py:15
  498.1 7.6 %all-to-all-start.6 = ((bf16[8,128,384]{1,2,0:T(8,128)(2,1)}), bf16[8,128,384]{1,2,0:T(8,128)(2,1)S(1)}, u32[]{:S(2)}, u32[]{:S(2)}) async-start(bf16[8,128,384]{1,2,0:T(8,128)(2,1)} %bitcast.82), calls=%async_computation.6 | async-start | bytes 1572864 | tf_op jit(solution)/shard_map/all_to_all | solution.py:216
  (225 shorter events, 206.2 us)
Async XLA Ops:
  3.0 17.2 %all-to-all-start.1 = ((bf16[128,8,384]{0,2,1:T(8,128)(2,1)}), bf16[128,8,384]{0,2,1:T(8,128)(2,1)S(1)}, u32[]{:S(2)}, u32[]{:S(2)}) async-start(bf16[128,8,384]{0,2,1:T(8,128)(2,1)} %bitcast.39), calls=%async_computation.1 | async-start | bytes 1572864 | tf_op jit(solution)/shard_map/all_to_all | solution.py:120
  20.2 15.8 %all-to-all-start.2 = ((bf16[128,8,384]{0,2,1:T(8,128)(2,1)}), bf16[128,8,384]{0,2,1:T(8,128)(2,1)S(1)}, u32[]{:S(2)}, u32[]{:S(2)}) async-start(bf16[128,8,384]{0,2,1:T(8,128)(2,1)} %bitcast.52), calls=%async_computation.2 | async-start | bytes 1572864 | tf_op jit(solution)/shard_map/all_to_all | solution.py:121
  25.2 50.6 %copy-start.10 = (s32[3,1,2]{2,0,1:T(4,128)}, s32[3,1,2]{2,0,1:T(4,128)S(1)}, u32[]{:S(2)}) copy-start(s32[3,1,2]{2,0,1:T(4,128)S(1)} %copy.131) | copy-start | bytes 76
  25.2 12.1 %copy-start.13 = (s32[8]{0:T(128)}, s32[8]{0:T(128)S(1)}, u32[]{:S(2)}) copy-start(s32[8]{0:T(128)S(1)} %iota_add_fusion) | copy-start | bytes 100
  37.9 1.8 collective-permute-start.2
  40.4 11.3 %collective-permute-start.3 = (bf16[2,3,2,128,128]{4,2,3,1,0:T(2,128)(2,1)S(1)}, bf16[2,3,2,128,128]{4,2,3,1,0:T(2,128)(2,1)}, u32[]{:S(2)}, u32[]{:S(2)}) collective-permute-start(bf16[2,3,2,128,128]{4,2,3,1,0:T(2,128)(2,1)S(1)} %fusion.97), channel_id=1, source_target_pairs={{0,16},{8,24},{16,0},{24,8},{32,48},{40,56},{48,32},{56,40},{64,80... | collective-permute-start | bytes 1179656 | tf_op jit(solution)/shard_map/ppermute | solution.py:25
  44.3 45.3 %all-to-all-start = ((bf16[128,8,384]{0,2,1:T(8,128)(2,1)}), bf16[128,8,384]{0,2,1:T(8,128)(2,1)S(1)}, u32[]{:S(2)}, u32[]{:S(2)}) async-start(bf16[128,8,384]{0,2,1:T(8,128)(2,1)} %bitcast.258), calls=%async_computation | async-start | bytes 1572864 | tf_op jit(solution)/shard_map/all_to_all | solution.py:119
  53.5 12.9 %collective-permute-start.4 = (bf16[2,3,2,128,128]{4,2,3,1,0:T(2,128)(2,1)S(1)}, bf16[2,3,2,128,128]{4,2,3,1,0:T(2,128)(2,1)}, u32[]{:S(2)}, u32[]{:S(2)}) collective-permute-start(bf16[2,3,2,128,128]{4,2,3,1,0:T(2,128)(2,1)S(1)} %fusion.104), channel_id=1, source_target_pairs={{0,32},{8,40},{16,48},{24,56},{32,0},{40,8},{48,16},{56,24},{64,96... | collective-permute-start | bytes 1179656 | tf_op jit(solution)/shard_map/ppermute | solution.py:25
  57.2 73.5 %collective-permute-start.8 = (bf16[1024,384]{1,0:T(8,128)(2,1)S(1)}, bf16[1024,384]{1,0:T(8,128)(2,1)}, u32[]{:S(2)}, u32[]{:S(2)}) collective-permute-start(bf16[1024,384]{1,0:T(8,128)(2,1)S(1)} %bitcast.254), channel_id=1, source_target_pairs={{8,0},{16,8},{24,16},{32,24},{40,32},{48,40},{56,48},{64,56},{72,6... | collective-permute-start | bytes 2359304 | tf_op jit(solution)/shard_map/ppermute | solution.py:15
  59.1 71.6 %collective-permute-start.7 = (bf16[1024,384]{1,0:T(8,128)(2,1)S(1)}, bf16[1024,384]{1,0:T(8,128)(2,1)}, u32[]{:S(2)}, u32[]{:S(2)}) collective-permute-start(bf16[1024,384]{1,0:T(8,128)(2,1)S(1)} %bitcast.255), channel_id=1, source_target_pairs={{0,8},{8,16},{16,24},{24,32},{32,40},{40,48},{48,56},{56,64},{64,7... | collective-permute-start | bytes 2359304 | tf_op jit(solution)/shard_map/ppermute | solution.py:15
  67.9 16.0 %collective-permute-start.5 = (bf16[2,3,2,128,128]{4,2,3,1,0:T(2,128)(2,1)S(1)}, bf16[2,3,2,128,128]{4,2,3,1,0:T(2,128)(2,1)S(1)}, u32[]{:S(2)}, u32[]{:S(2)}) collective-permute-start(bf16[2,3,2,128,128]{4,2,3,1,0:T(2,128)(2,1)S(1)} %add.99), channel_id=1, source_target_pairs={{0,64},{8,72},{16,80},{24,88},{32,96},{40,104},{48,112},{56,120},{... | collective-permute-start | bytes 1179656 | tf_op jit(solution)/shard_map/ppermute | solution.py:25
  70.6 69.1 %collective-permute-start.1 = (bf16[1024,384]{1,0:T(8,128)(2,1)}, bf16[1024,384]{1,0:T(8,128)(2,1)}, u32[]{:S(2)}, u32[]{:S(2)}) collective-permute-start(bf16[1024,384]{1,0:T(8,128)(2,1)} %bitcast.41), channel_id=1, source_target_pairs={{8,0},{16,8},{24,16},{32,24},{40,32},{48,40},{56,48},{64,56},{72,6... | collective-permute-start | bytes 2359304 | tf_op jit(solution)/shard_map/ppermute | solution.py:15
  72.5 67.2 %collective-permute-start = (bf16[1024,384]{1,0:T(8,128)(2,1)}, bf16[1024,384]{1,0:T(8,128)(2,1)}, u32[]{:S(2)}, u32[]{:S(2)}) collective-permute-start(bf16[1024,384]{1,0:T(8,128)(2,1)} %bitcast.41), channel_id=1, source_target_pairs={{0,8},{8,16},{16,24},{24,32},{32,40},{40,48},{48,56},{56,64},{64,7... | collective-permute-start | bytes 2359304 | tf_op jit(solution)/shard_map/ppermute | solution.py:15
  84.3 65.9 %collective-permute-start.6 = (bf16[2,3,2,128,128]{4,2,3,1,0:T(2,128)(2,1)S(1)}, bf16[2,3,2,128,128]{4,2,3,1,0:T(2,128)(2,1)}, u32[]{:S(2)}, u32[]{:S(2)}) collective-permute-start(bf16[2,3,2,128,128]{4,2,3,1,0:T(2,128)(2,1)S(1)} %add.100), channel_id=1, source_target_pairs={{0,128},{8,136},{16,144},{24,152},{32,160},{40,168},{48,176},{56,1... | collective-permute-start | bytes 1179656 | tf_op jit(solution)/shard_map/ppermute | solution.py:25
  89.6 104.1 %all-to-all-start.4 = ((bf16[128,8,384]{0,2,1:T(8,128)(2,1)}), bf16[128,8,384]{0,2,1:T(8,128)(2,1)}, u32[]{:S(2)}, u32[]{:S(2)}) async-start(bf16[128,8,384]{0,2,1:T(8,128)(2,1)} %bitcast.70), calls=%async_computation.4 | async-start | bytes 1572864 | tf_op jit(solution)/shard_map/all_to_all | solution.py:122
  312.2 2.4 collective-permute-start.11
  316.0 19.8 %collective-permute-start.12 = (f32[2,3,2,128,128]{4,2,3,1,0:T(2,128)}, f32[2,3,2,128,128]{4,2,3,1,0:T(2,128)S(1)}, u32[]{:S(2)}, u32[]{:S(2)}) collective-permute-start(f32[2,3,2,128,128]{4,2,3,1,0:T(2,128)} %fusion.98), channel_id=1, source_target_pairs={{0,16},{8,24},{16,0},{24,8},{32,48},{40,56},{48,32},{56,40},{64,80... | collective-permute-start | bytes 2359304 | tf_op jit(solution)/shard_map/ppermute | solution.py:25
  317.2 48.7 %all-to-all-start.3 = ((bf16[8,128,384]{1,2,0:T(8,128)(2,1)}), bf16[8,128,384]{1,2,0:T(8,128)(2,1)}, u32[]{:S(2)}, u32[]{:S(2)}) async-start(bf16[8,128,384]{1,2,0:T(8,128)(2,1)} %bitcast.65), calls=%async_computation.3 | async-start | bytes 1572864 | tf_op jit(solution)/shard_map/all_to_all | solution.py:214
  336.5 21.0 %collective-permute-start.13 = (f32[2,3,2,128,128]{4,2,3,1,0:T(2,128)S(1)}, f32[2,3,2,128,128]{4,2,3,1,0:T(2,128)S(1)}, u32[]{:S(2)}, u32[]{:S(2)}) collective-permute-start(f32[2,3,2,128,128]{4,2,3,1,0:T(2,128)S(1)} %fusion.103), channel_id=1, source_target_pairs={{0,32},{8,40},{16,48},{24,56},{32,0},{40,8},{48,16},{56,24},{64,96... | collective-permute-start | bytes 2359304 | tf_op jit(solution)/shard_map/ppermute | solution.py:25
  358.8 36.2 %collective-permute-start.14 = (f32[2,3,2,128,128]{4,2,3,1,0:T(2,128)}, f32[2,3,2,128,128]{4,2,3,1,0:T(2,128)}, u32[]{:S(2)}, u32[]{:S(2)}) collective-permute-start(f32[2,3,2,128,128]{4,2,3,1,0:T(2,128)} %add.108), channel_id=1, source_target_pairs={{0,64},{8,72},{16,80},{24,88},{32,96},{40,104},{48,112},{56,120},{... | collective-permute-start | bytes 2359304 | tf_op jit(solution)/shard_map/ppermute | solution.py:25
  365.8 92.4 %all-to-all-start.5 = ((bf16[8,128,384]{1,2,0:T(8,128)(2,1)}), bf16[8,128,384]{1,2,0:T(8,128)(2,1)}, u32[]{:S(2)}, u32[]{:S(2)}) async-start(bf16[8,128,384]{1,2,0:T(8,128)(2,1)} %bitcast.261), calls=%async_computation.5 | async-start | bytes 1572864 | tf_op jit(solution)/shard_map/all_to_all | solution.py:215
  396.7 28.6 %collective-permute-start.15 = (f32[2,3,2,128,128]{4,2,3,1,0:T(2,128)S(1)}, f32[2,3,2,128,128]{4,2,3,1,0:T(2,128)S(1)}, u32[]{:S(2)}, u32[]{:S(2)}) collective-permute-start(f32[2,3,2,128,128]{4,2,3,1,0:T(2,128)S(1)} %add.109), channel_id=1, source_target_pairs={{0,128},{8,136},{16,144},{24,152},{32,160},{40,168},{48,176},{56,1... | collective-permute-start | bytes 2359304 | tf_op jit(solution)/shard_map/ppermute | solution.py:25
  398.4 42.4 %collective-permute-start.16 = (bf16[3,8,128,128]{3,1,2,0:T(8,128)(2,1)S(1)}, bf16[3,8,128,128]{3,1,2,0:T(8,128)(2,1)S(1)}, u32[]{:S(2)}, u32[]{:S(2)}) collective-permute-start(bf16[3,8,128,128]{3,1,2,0:T(8,128)(2,1)S(1)} %get-tuple-element.221), channel_id=1, source_target_pairs={{8,0},{16,8},{24,16},{32,24},{40,32},{48,40},{56,48},{64,56},{72,6... | collective-permute-start | bytes 2359304 | tf_op jit(solution)/shard_map/ppermute | solution.py:15
  406.9 45.2 %copy-start.11 = (s32[3,1,2]{2,0,1:T(4,128)S(1)}, s32[3,1,2]{2,0,1:T(4,128)}, u32[]{:S(2)}) copy-start(s32[3,1,2]{2,0,1:T(4,128)} %copy-done.10) | copy-start | bytes 76
  406.9 45.2 %copy-start.14 = (s32[8]{0:T(128)S(1)}, s32[8]{0:T(128)}, u32[]{:S(2)}) copy-start(s32[8]{0:T(128)} %copy-done.13) | copy-start | bytes 100
  406.9 45.2 %collective-permute-start.17 = (bf16[3,8,128,128]{3,1,2,0:T(8,128)(2,1)S(1)}, bf16[3,8,128,128]{3,1,2,0:T(8,128)(2,1)S(1)}, u32[]{:S(2)}, u32[]{:S(2)}) collective-permute-start(bf16[3,8,128,128]{3,1,2,0:T(8,128)(2,1)S(1)} %get-tuple-element.222), channel_id=1, source_target_pairs={{0,8},{8,16},{16,24},{24,32},{32,40},{40,48},{48,56},{56,64},{64,7... | collective-permute-start | bytes 2359304 | tf_op jit(solution)/shard_map/ppermute | solution.py:15
  425.8 26.4 %copy-start.7 = (f32[2,3,2,128,128]{4,2,3,1,0:T(2,128)}, f32[2,3,2,128,128]{4,2,3,1,0:T(2,128)S(1)}, u32[]{:S(2)}) copy-start(f32[2,3,2,128,128]{4,2,3,1,0:T(2,128)S(1)} %add.110) | copy-start | bytes 2359300
  458.2 39.9 %all-to-all-start.7 = ((bf16[8,128,384]{1,2,0:T(8,128)(2,1)}), bf16[8,128,384]{1,2,0:T(8,128)(2,1)}, u32[]{:S(2)}, u32[]{:S(2)}) async-start(bf16[8,128,384]{1,2,0:T(8,128)(2,1)} %bitcast.259), calls=%async_computation.7 | async-start | bytes 1572864 | tf_op jit(solution)/shard_map/all_to_all | solution.py:217
  465.1 28.9 %copy-start.8 = (f32[2,3,2,128,128]{4,2,3,1,0:T(2,128)S(1)}, f32[2,3,2,128,128]{4,2,3,1,0:T(2,128)}, u32[]{:S(2)}) copy-start(f32[2,3,2,128,128]{4,2,3,1,0:T(2,128)} %copy-done.7) | copy-start | bytes 2359300
  465.4 14.9 %collective-permute-start.9 = (bf16[3,8,128,128]{3,1,2,0:T(8,128)(2,1)S(1)}, bf16[3,8,128,128]{3,1,2,0:T(8,128)(2,1)S(1)}, u32[]{:S(2)}, u32[]{:S(2)}) collective-permute-start(bf16[3,8,128,128]{3,1,2,0:T(8,128)(2,1)S(1)} %get-tuple-element.223), channel_id=1, source_target_pairs={{8,0},{16,8},{24,16},{32,24},{40,32},{48,40},{56,48},{64,56},{72,6... | collective-permute-start | bytes 2359304 | tf_op jit(solution)/shard_map/ppermute | solution.py:15
  469.0 25.0 %collective-permute-start.10 = (bf16[3,8,128,128]{3,1,2,0:T(8,128)(2,1)S(1)}, bf16[3,8,128,128]{3,1,2,0:T(8,128)(2,1)S(1)}, u32[]{:S(2)}, u32[]{:S(2)}) collective-permute-start(bf16[3,8,128,128]{3,1,2,0:T(8,128)(2,1)S(1)} %get-tuple-element.224), channel_id=1, source_target_pairs={{0,8},{8,16},{16,24},{24,32},{32,40},{40,48},{48,56},{56,64},{64,7... | collective-permute-start | bytes 2359304 | tf_op jit(solution)/shard_map/ppermute | solution.py:15
  498.1 16.2 %all-to-all-start.6 = ((bf16[8,128,384]{1,2,0:T(8,128)(2,1)}), bf16[8,128,384]{1,2,0:T(8,128)(2,1)S(1)}, u32[]{:S(2)}, u32[]{:S(2)}) async-start(bf16[8,128,384]{1,2,0:T(8,128)(2,1)} %bitcast.82), calls=%async_computation.6 | async-start | bytes 1572864 | tf_op jit(solution)/shard_map/all_to_all | solution.py:216
  (19 other events, 66.5 us)

commit v2 on v1

v2 whole, which is shorter than its diff:
```python
import jax
import jax.numpy as jnp
from jax import lax
from jax.experimental import pallas as pl
from jax.experimental.pallas import tpu as pltpu
from jax.sharding import PartitionSpec as P

HD = 128
TILE = 128
GLOBALS = 2
HALF = 8


def passed_along(block, axis, distance):
    devices = range(lax.axis_size(axis))
    route = [(i - distance, i) for i in devices if i - distance in devices]
    return lax.ppermute(block, axis, route)


def butterfly_sum(block, axis):
    count = lax.axis_size(axis)
    if count & (count - 1):
        return lax.psum(block, axis)
    stride = 1
    while stride < count:
        route = [(i, i ^ stride) for i in range(count)]
        block = block + lax.ppermute(block, axis, route)
        stride *= 2
    return block


def split_heads(field, count):
    heads = field.shape[1] // HD
    return field.reshape(count, TILE, heads, HD).transpose(2, 0, 1, 3)


def merge_heads(field):
    heads = field.shape[0]
    count = field.shape[1]
    return field.transpose(1, 2, 0, 3).reshape(count * TILE, heads * HD)


def attention_kernel(index_ref, q_ref, do_ref, k_ref, v_ref, att_ref, dq_ref, dk_ref, dv_ref, kbuf, vbuf):
    heads = q_ref.shape[1] // HD
    tiles = q_ref.shape[0] // TILE
    slots = index_ref.shape[0] // (heads * tiles)
    scale = HD ** (-0.5)
    dk_ref[...] = jnp.zeros_like(dk_ref)
    dv_ref[...] = jnp.zeros_like(dv_ref)
    nt = (((1,), (1,)), ((), ()))
    tn = (((0,), (0,)), ((), ()))

    def step(item, carry):
        head = item // tiles
        tile = item % tiles
        cols = pl.ds(pl.multiple_of(head * HD, HD), HD)
        rows = pl.ds(pl.multiple_of(tile * TILE, TILE), TILE)
        picks = [
            pl.ds(pl.multiple_of(index_ref[item * slots + s] * TILE, TILE), TILE)
            for s in range(slots)
        ]
        for s in range(slots):
            kbuf[s * TILE : (s + 1) * TILE, :] = k_ref[picks[s], cols]
            vbuf[s * TILE : (s + 1) * TILE, :] = v_ref[picks[s], cols]
        query = q_ref[rows, cols]
        grad_out = do_ref[rows, cols]
        chosen_keys = kbuf[...]
        chosen_values = vbuf[...]
        scores = (
            lax.dot_general(query, chosen_keys, nt, preferred_element_type=jnp.float32) * scale
        )
        peak = jnp.max(scores, axis=1, keepdims=True)
        log_total = peak + jnp.log(jnp.sum(jnp.exp(scores - peak), axis=1, keepdims=True))
        probs = jnp.exp(scores - log_total)
        weights = probs.astype(jnp.bfloat16)
        attended = jnp.dot(weights, chosen_values, preferred_element_type=jnp.float32).astype(
            jnp.bfloat16
        )
        att_ref[rows, cols] = attended
        delta = jnp.sum(
            grad_out.astype(jnp.float32) * attended.astype(jnp.float32), axis=1, keepdims=True
        )
        grad_probs = lax.dot_general(
            grad_out, chosen_values, nt, preferred_element_type=jnp.float32
        )
        grad_scores = (probs * (grad_probs - delta)).astype(jnp.bfloat16)
        dq_ref[rows, cols] = (
            jnp.dot(grad_scores, chosen_keys, preferred_element_type=jnp.float32) * scale
        ).astype(jnp.bfloat16)
        key_slots = (
            lax.dot_general(grad_scores, query, tn, preferred_element_type=jnp.float32) * scale
        )
        value_slots = lax.dot_general(weights, grad_out, tn, preferred_element_type=jnp.float32)
        for s in range(slots):
            dk_ref[picks[s], cols] += key_slots[s * TILE : (s + 1) * TILE]
            dv_ref[picks[s], cols] += value_slots[s * TILE : (s + 1) * TILE]
        return carry

    lax.fori_loop(0, heads * tiles, step, 0)


def attend(pool_index, query_rows, grad_rows, pool_keys, pool_values):
    count, width = query_rows.shape
    pool_rows = pool_keys.shape[0]
    slots = pool_index.shape[-1]
    vmem = pltpu.VMEM
    flops = 2 * 7 * count * slots * TILE * width
    return pl.pallas_call(
        attention_kernel,
        out_shape=(
            jax.ShapeDtypeStruct((count, width), jnp.bfloat16),
            jax.ShapeDtypeStruct((count, width), jnp.bfloat16),
            jax.ShapeDtypeStruct((pool_rows, width), jnp.float32),
            jax.ShapeDtypeStruct((pool_rows, width), jnp.float32),
        ),
        in_specs=[pl.BlockSpec(memory_space=pltpu.SMEM)] + [pl.BlockSpec(memory_space=vmem)] * 4,
        out_specs=tuple(pl.BlockSpec(memory_space=vmem) for _ in range(4)),
        scratch_shapes=[
            pltpu.VMEM((slots * TILE, HD), jnp.bfloat16),
            pltpu.VMEM((slots * TILE, HD), jnp.bfloat16),
        ],
        compiler_params=pltpu.CompilerParams(vmem_limit_bytes=60 * 1024 * 1024),
        cost_estimate=pl.CostEstimate(
            flops=flops,
            transcendentals=count * slots * TILE * width // HD,
            bytes_accessed=8 * count * width + 12 * pool_rows * width,
        ),
    )(pool_index.reshape(-1), query_rows, grad_rows, pool_keys, pool_values)


def per_device(query, keys, values, cotangent, kv_tiles):
    head_count = lax.axis_size("head")
    cycle_pos = lax.axis_index("blk")
    per_frame = query.shape[0] * head_count // TILE
    reach = -(-HALF // per_frame)
    span = (2 * reach + 1) * per_frame
    global_tiles = kv_tiles[:, 0, :GLOBALS]
    own_tiles = lax.dynamic_slice_in_dim(kv_tiles, cycle_pos * per_frame, per_frame, 1)
    moved = (
        lax.all_to_all(query, "head", split_axis=1, concat_axis=0, tiled=True),
        lax.all_to_all(keys, "head", split_axis=1, concat_axis=0, tiled=True),
        lax.all_to_all(values, "head", split_axis=1, concat_axis=0, tiled=True),
        lax.all_to_all(cotangent, "head", split_axis=1, concat_axis=0, tiled=True),
    )
    frame_keys = moved[1]
    frame_values = moved[2]
    offset = 1
    earlier = passed_along((frame_keys, frame_values), "blk", offset)
    later = passed_along((frame_keys, frame_values), "blk", -offset)
    earlier_keys = [earlier[0]]
    earlier_values = [earlier[1]]
    later_keys = [later[0]]
    later_values = [later[1]]
    near_keys = jnp.stack(earlier_keys[::-1] + later_keys, axis=0)
    near_values = jnp.stack(earlier_values[::-1] + later_values, axis=0)
    width = frame_keys.shape[1]
    all_keys = jnp.concatenate(
        [near_keys[:reach], frame_keys[None], near_keys[reach:]], axis=0
    ).reshape(span * TILE, width)
    all_values = jnp.concatenate(
        [near_values[:reach], frame_values[None], near_values[reach:]], axis=0
    ).reshape(span * TILE, width)
    heads = width // HD
    tile_ids = cycle_pos * per_frame + jnp.arange(per_frame, dtype=jnp.int32)
    owner = global_tiles[:, :, None] == tile_ids[None, None, :]
    owner_mask = owner.astype(jnp.bfloat16)
    frame_key_tiles = frame_keys.reshape(per_frame, TILE, heads, HD)
    frame_value_tiles = frame_values.reshape(per_frame, TILE, heads, HD)
    global_keys = jnp.einsum(
        "hjt,tkhd->jkhd", owner_mask, frame_key_tiles, preferred_element_type=jnp.float32
    )
    global_values = jnp.einsum(
        "hjt,tkhd->jkhd", owner_mask, frame_value_tiles, preferred_element_type=jnp.float32
    )
    global_both = butterfly_sum(
        jnp.stack([global_keys.astype(jnp.bfloat16), global_values.astype(jnp.bfloat16)]), "blk"
    )
    global_rows = GLOBALS * TILE
    pool_keys = jnp.concatenate([all_keys, global_both[0].reshape(global_rows, width)], axis=0)
    pool_values = jnp.concatenate([all_values, global_both[1].reshape(global_rows, width)], axis=0)
    relative = own_tiles - (cycle_pos - reach) * per_frame
    inside = (relative >= 0) & (relative < span)
    matches = own_tiles[:, :, :, None] == global_tiles[:, None, None, :]
    slot_numbers = jnp.arange(global_tiles.shape[1], dtype=jnp.int32)
    global_slot = jnp.sum(jnp.where(matches, slot_numbers[None, None, None, :], 0), axis=-1)
    pool_index = jnp.where(inside, relative, span + global_slot)
    attended, query_rows, key_pool, value_pool = attend(
        pool_index, moved[0], moved[3], pool_keys, pool_values
    )
    frame_rows = per_frame * TILE
    centre = reach * frame_rows
    key_grad = key_pool[centre : centre + frame_rows]
    value_grad = value_pool[centre : centre + frame_rows]
    offset = 1
    lower = (reach - offset) * frame_rows
    returned = (
        passed_along(
            key_pool[lower : lower + frame_rows].astype(jnp.bfloat16), "blk", -offset
        ).astype(jnp.float32),
        passed_along(
            value_pool[lower : lower + frame_rows].astype(jnp.bfloat16), "blk", -offset
        ).astype(jnp.float32),
    )
    key_grad = key_grad + returned[0]
    value_grad = value_grad + returned[1]
    upper = (reach + offset) * frame_rows
    returned = (
        passed_along(
            key_pool[upper : upper + frame_rows].astype(jnp.bfloat16), "blk", offset
        ).astype(jnp.float32),
        passed_along(
            value_pool[upper : upper + frame_rows].astype(jnp.bfloat16), "blk", offset
        ).astype(jnp.float32),
    )
    key_grad = key_grad + returned[0]
    value_grad = value_grad + returned[1]
    pool_end = span * TILE
    summed = butterfly_sum(
        jnp.stack([key_pool[pool_end:], value_pool[pool_end:]]).reshape(
            2, GLOBALS, TILE, heads, HD
        ),
        "blk",
    )
    owner_float = owner.astype(jnp.float32)
    key_grad = key_grad + jnp.einsum(
        "hjt,jkhd->tkhd", owner_float, summed[0], precision=lax.Precision.HIGHEST
    ).reshape(frame_rows, width)
    value_grad = value_grad + jnp.einsum(
        "hjt,jkhd->tkhd", owner_float, summed[1], precision=lax.Precision.HIGHEST
    ).reshape(frame_rows, width)
    key_rows = key_grad.astype(jnp.bfloat16)
    value_rows = value_grad.astype(jnp.bfloat16)
    results = (
        lax.all_to_all(attended, "head", split_axis=0, concat_axis=1, tiled=True),
        lax.all_to_all(query_rows, "head", split_axis=0, concat_axis=1, tiled=True),
        lax.all_to_all(key_rows, "head", split_axis=0, concat_axis=1, tiled=True),
        lax.all_to_all(value_rows, "head", split_axis=0, concat_axis=1, tiled=True),
    )
    return (results[0], results[1], results[2], results[3])


def solution(mesh):
    placed = (
        P(("blk", "head"), None),
        P(("blk", "head"), None),
        P(("blk", "head"), None),
        P(("blk", "head"), None),
        P("head", None, None),
    )
    return jax.shard_map(
        per_device,
        mesh=mesh,
        in_specs=placed,
        out_specs=(
            P(("blk", "head"), None),
            P(("blk", "head"), None),
            P(("blk", "head"), None),
            P(("blk", "head"), None),
        ),
        check_vma=False,
    )
```

time: 526 us -> 392 us (0.75); the launches traced: 516 us -> 388 us
  matrix products: 93 us -> 2.77 us
  local copies, waits for them, and re-layouts: 92.6 us -> 23.9 us
  Pallas kernels: 0 us -> 36.7 us
  loops' own time: 11.3 us -> 0 us
  starting transfers between devices: 122 us -> 130 us
  other arithmetic: 36.2 us -> 29.4 us
    dot_general x31 -> x4, matrix products: 93 us -> 2.77 us  [the longest x1 0.97 us: per_device(): jnp.einsum('hjt,jkhd->tkhd', owner_float, summed[1], precision=lax.Precis...]
    pallas_call x0 -> x1, Pallas kernels: none -> 36.7 us  [attend(): pl.pallas_call(attention_kernel, out_shape=(jax.ShapeDtypeStruct((count,...]
    gather x12 -> x0, local copies, waits for them, and re-layouts: 25.2 us -> none  [the longest x3 7.48 us: attend_forward(): chosen_values = jnp.take(pool_values, pool_index, axis=0)]
    another operation x3 -> x5, local copies, waits for them, and re-layouts: 15.1 us -> 0.99 us  [the longest x3 0.65 us: per_device(): jnp.stack([key_pool[pool_end:], value_pool[pool_end:]])]
    unnamed x29 -> x18, local copies, waits for them, and re-layouts: 16.4 us -> 4.87 us
    another operation x2 -> x0, loops' own time: 11.3 us -> none  [the longest x1 11.2 us: per_device(): lax.map(attend_backward, (queries, pool_keys, pool_values, grad_out, atte...]
    while x34 -> x0, local copies, waits for them, and re-layouts: 10.8 us -> none  [the longest x4 6.71 us: per_device(): lax.map(attend_forward, (queries, pool_keys, pool_values, pool_index))]
    all_to_all x0 -> x6, local copies, waits for them, and re-layouts: none -> 9.34 us  [the longest x1 2.13 us: per_device(): lax.all_to_all(query_rows, 'head', split_axis=0, concat_axis=1, tiled=True)]
  transfers between devices with their start and end apart: 26 -> 26, of which waited for: 16 -> 17; matrix products, arithmetic and copies ran while one was open for 20% -> 12% of each run, Pallas kernels for 0% -> 0%
where the time goes in v2:
time: 392 us; the launch traced here: 388 us
  waiting for transfers between devices  164 us (42%)
  starting transfers between devices  130 us (33%)
  Pallas kernels  36.7 us (9%)
  other arithmetic  29.4 us (8%)
  local copies, waits for them, and re-layouts  23.9 us (6%)
    ppermute x10, waiting for transfers between devices, butterfly_sum(): block = block + lax.ppermute(block, axis, route)  88.2 us
    ppermute x8, waiting for transfers between devices, passed_along(): return lax.ppermute(block, axis, route)  47.2 us
    all_to_all x1, starting transfers between devices, per_device(): lax.all_to_all(cotangent, 'head', split_axis=1, concat_axis=0, tiled=True)  41.8 us
    pallas_call x1, Pallas kernels, attend(): pl.pallas_call(attention_kernel, out_shape=(jax.ShapeDtypeStruct((count,...  36.7 us
    ppermute x8, starting transfers between devices, passed_along(): return lax.ppermute(block, axis, route)  28.4 us
    ppermute x10, starting transfers between devices, butterfly_sum(): block = block + lax.ppermute(block, axis, route)  17.4 us
    all_to_all x1, waiting for transfers between devices, per_device(): lax.all_to_all(keys, 'head', split_axis=1, concat_axis=0, tiled=True)  10.4 us
    all_to_all x1, waiting for transfers between devices, per_device(): lax.all_to_all(values, 'head', split_axis=1, concat_axis=0, tiled=True)  10.3 us
  transfers between devices with their start and end apart: 26, of which 17 were waited for; matrix products, arithmetic and copies ran while one was open for 12% of the time, Pallas kernels for 0%

profile of v2, /device:TPU:160, one launch (start us, length us, event | category | flops | bytes accessed | tf_op | source)
XLA Modules:
  0.0 387.7 jit_solution(10495510090923896816)
XLA Ops:
  3.0 5.8 %all-to-all-start.3 = ((bf16[128,8,384]{0,2,1:T(8,128)(2,1)}), bf16[128,8,384]{0,2,1:T(8,128)(2,1)S(1)}, u32[]{:S(2)}, u32[]{:S(2)}) async-start(bf16[128,8,384]{0,2,1:T(8,128)(2,1)} %bitcast.17), calls=%async_computation.3 | async-start | bytes 1572864 | tf_op jit(solution)/shard_map/all_to_all | solution.py:142
  9.9 10.3 %all-to-all-done.3 = bf16[128,8,384]{0,2,1:T(8,128)(2,1)S(1)} async-done(((bf16[128,8,384]{0,2,1:T(8,128)(2,1)}), bf16[128,8,384]{0,2,1:T(8,128)(2,1)S(1)}, u32[]{:S(2)}, u32[]{:S(2)}) %all-to-all-start.3) | async-done | bytes 786464 | tf_op jit(solution)/shard_map/all_to_all | solution.py:142
  20.2 4.2 %all-to-all-start.2 = ((bf16[128,8,384]{0,2,1:T(8,128)(2,1)}), bf16[128,8,384]{0,2,1:T(8,128)(2,1)S(1)}, u32[]{:S(2)}, u32[]{:S(2)}) async-start(bf16[128,8,384]{0,2,1:T(8,128)(2,1)} %bitcast.4), calls=%async_computation.2 | async-start | bytes 1572864 | tf_op jit(solution)/shard_map/all_to_all | solution.py:141
  25.6 10.4 %all-to-all-done.2 = bf16[128,8,384]{0,2,1:T(8,128)(2,1)S(1)} async-done(((bf16[128,8,384]{0,2,1:T(8,128)(2,1)}), bf16[128,8,384]{0,2,1:T(8,128)(2,1)S(1)}, u32[]{:S(2)}, u32[]{:S(2)}) %all-to-all-start.2) | async-done | bytes 786464 | tf_op jit(solution)/shard_map/all_to_all | solution.py:141
  43.0 4.7 %all-to-all-start = ((bf16[128,8,384]{2,0,1:T(8,128)(2,1)}), bf16[128,8,384]{2,0,1:T(8,128)(2,1)}, u32[]{:S(2)}, u32[]{:S(2)}) async-start(bf16[128,8,384]{2,0,1:T(8,128)(2,1)} %bitcast.99), calls=%async_computation | async-start | bytes 1572864 | tf_op jit(solution)/shard_map/all_to_all | solution.py:140
  47.7 3.9 %collective-permute-done.3 = bf16[2,2,128,3,128]{4,1,2,3,0:T(2,128)(2,1)S(1)} collective-permute-done((bf16[2,2,128,3,128]{4,1,2,3,0:T(2,128)(2,1)S(1)}, bf16[2,2,128,3,128]{4,1,2,3,0:T(2,128)(2,1)S(1)}, u32[]{:S(2)}, u32[]{:S(2)}) %collective-permute-start.3) | collective-permute-done | bytes 393248 | tf_op jit(solution)/shard_map/ppermute | solution.py:27
  52.4 3.3 collective-permute-start.4
  60.4 5.0 %collective-permute-done.4 = bf16[2,2,128,3,128]{4,1,2,3,0:T(2,128)(2,1)S(1)} collective-permute-done((bf16[2,2,128,3,128]{4,1,2,3,0:T(2,128)(2,1)S(1)}, bf16[2,2,128,3,128]{4,1,2,3,0:T(2,128)(2,1)S(1)}, u32[]{:S(2)}, u32[]{:S(2)}) %collective-permute-start.4) | collective-permute-done | bytes 393248 | tf_op jit(solution)/shard_map/ppermute | solution.py:27
  75.7 6.0 %collective-permute-done.5 = bf16[2,2,128,3,128]{4,1,2,3,0:T(2,128)(2,1)} collective-permute-done((bf16[2,2,128,3,128]{4,1,2,3,0:T(2,128)(2,1)S(1)}, bf16[2,2,128,3,128]{4,1,2,3,0:T(2,128)(2,1)}, u32[]{:S(2)}, u32[]{:S(2)}) %collective-permute-start.5) | collective-permute-done | bytes 393248 | tf_op jit(solution)/shard_map/ppermute | solution.py:27
  85.1 41.8 %all-to-all-start.1 = ((bf16[128,8,384]{2,0,1:T(8,128)(2,1)}), bf16[128,8,384]{2,0,1:T(8,128)(2,1)}, u32[]{:S(2)}, u32[]{:S(2)}) async-start(bf16[128,8,384]{2,0,1:T(8,128)(2,1)} %bitcast.98), calls=%async_computation.1 | async-start | bytes 1572864 | tf_op jit(solution)/shard_map/all_to_all | solution.py:143
  132.7 5.4 %pad_maximum_fusion = (bf16[3328,384]{1,0:T(8,128)(2,1)}, bf16[3328,384]{1,0:T(8,128)(2,1)}) fusion(bf16[256,384]{1,0:T(8,128)(2,1)S(1)} %bitcast.129, bf16[3072,384]{1,0:T(8,128)(2,1)S(1)} %bitcast.102, bf16[256,384]{1,0:T(8,128)(2,1)S(1)} %bitcast.130, bf16[3072,384]{1,0:T(8,128)(2,1)S(1)} %bitcast.103), kind=kLoop, calls=%fused_computation | loop fusion | flops 10223616 | bytes 10223616 | tf_op jit(solution)/shard_map/concatenate | solution.py:179
  138.0 4.9 %all-to-all-done.1 = bf16[128,8,384]{2,0,1:T(8,128)(2,1)} async-done(((bf16[128,8,384]{2,0,1:T(8,128)(2,1)}), bf16[128,8,384]{2,0,1:T(8,128)(2,1)}, u32[]{:S(2)}, u32[]{:S(2)}) %all-to-all-start.1) | async-done | bytes 786464 | tf_op jit(solution)/shard_map/all_to_all | solution.py:143
  142.9 36.7 %shard_map.84 = (bf16[1024,384]{1,0:T(8,128)(2,1)}, bf16[1024,384]{1,0:T(8,128)(2,1)}, f32[3328,384]{1,0:T(8,128)}, f32[3328,384]{1,0:T(8,128)}) custom-call(s32[216]{0:T(256)} %reshape.69.index_ref, bf16[1024,384]{1,0:T(8,128)(2,1)} %bitcast.1.q_ref, bf16[1024,384]{1,0:T(8,128)(2,1)} %bitcast.3.do_ref, bf16[3328,384]{1,0:T(8,128)(2,1)} %get-tuple-element.18.k_ref, ...), custom_call_target="tpu_custom_call" | custom-call | flops 6341787648 | bytes 18481152 | tf_op jit(solution)/shard_map/pallas_call | solution.py:108
  185.5 19.6 %collective-permute-done.12 = f32[2,2,128,3,128]{4,1,2,3,0:T(2,128)S(1)} collective-permute-done((f32[2,2,128,3,128]{4,1,2,3,0:T(2,128)S(1)}, f32[2,2,128,3,128]{4,1,2,3,0:T(2,128)S(1)}, u32[]{:S(2)}, u32[]{:S(2)}) %collective-permute-start.12) | collective-permute-done | bytes 786464 | tf_op jit(solution)/shard_map/ppermute | solution.py:27
  208.1 6.1 %all-to-all-start.4 = ((bf16[8,128,384]{2,1,0:T(8,128)(2,1)}), bf16[8,128,384]{2,1,0:T(8,128)(2,1)S(1)}, u32[]{:S(2)}, u32[]{:S(2)}) async-start(bf16[8,128,384]{2,1,0:T(8,128)(2,1)} %bitcast.27), calls=%async_computation.4 | async-start | bytes 1572864 | tf_op jit(solution)/shard_map/all_to_all | solution.py:234
  214.2 11.6 %collective-permute-done.13 = f32[2,2,128,3,128]{4,1,2,3,0:T(2,128)S(1)} collective-permute-done((f32[2,2,128,3,128]{4,1,2,3,0:T(2,128)S(1)}, f32[2,2,128,3,128]{4,1,2,3,0:T(2,128)S(1)}, u32[]{:S(2)}, u32[]{:S(2)}) %collective-permute-start.13) | collective-permute-done | bytes 786464 | tf_op jit(solution)/shard_map/ppermute | solution.py:27
  226.2 3.8 collective-permute-start.14
  232.8 30.3 %collective-permute-done.14 = f32[2,2,128,3,128]{4,1,2,3,0:T(2,128)S(1)} collective-permute-done((f32[2,2,128,3,128]{4,1,2,3,0:T(2,128)S(1)}, f32[2,2,128,3,128]{4,1,2,3,0:T(2,128)S(1)}, u32[]{:S(2)}, u32[]{:S(2)}) %collective-permute-start.14) | collective-permute-done | bytes 786464 | tf_op jit(solution)/shard_map/ppermute | solution.py:27
  266.5 7.8 %all-to-all-start.5 = ((bf16[8,128,384]{2,1,0:T(8,128)(2,1)}), bf16[8,128,384]{2,1,0:T(8,128)(2,1)}, u32[]{:S(2)}, u32[]{:S(2)}) async-start(bf16[8,128,384]{2,1,0:T(8,128)(2,1)} %bitcast.124), calls=%async_computation.5 | async-start | bytes 1572864 | tf_op jit(solution)/shard_map/all_to_all | solution.py:235
  276.4 7.9 %collective-permute-start.9 = (bf16[1024,384]{1,0:T(8,128)(2,1)S(1)}, bf16[1024,384]{1,0:T(8,128)(2,1)S(1)}, u32[]{:S(2)}, u32[]{:S(2)}) collective-permute-start(bf16[1024,384]{1,0:T(8,128)(2,1)S(1)} %get-tuple-element.14), channel_id=1, source_target_pairs={{8,0},{16,8},{24,16},{32,24},{40,32},{48,40},{56,48},{64,56},{72,6... | collective-permute-start | bytes 2359304 | tf_op jit(solution)/shard_map/ppermute | solution.py:17
  284.3 2.7 convert.9
  287.0 7.9 %collective-permute-done.15 = f32[2,2,128,3,128]{4,1,2,3,0:T(2,128)} collective-permute-done((f32[2,2,128,3,128]{4,1,2,3,0:T(2,128)}, f32[2,2,128,3,128]{4,1,2,3,0:T(2,128)}, u32[]{:S(2)}, u32[]{:S(2)}) %collective-permute-start.15) | collective-permute-done | bytes 786464 | tf_op jit(solution)/shard_map/ppermute | solution.py:27
  299.6 13.5 %collective-permute-done.10 = bf16[1024,384]{1,0:T(8,128)(2,1)S(1)} collective-permute-done((bf16[1024,384]{1,0:T(8,128)(2,1)S(1)}, bf16[1024,384]{1,0:T(8,128)(2,1)S(1)}, u32[]{:S(2)}, u32[]{:S(2)}) %collective-permute-start.10) | collective-permute-done | bytes 786464 | tf_op jit(solution)/shard_map/ppermute | solution.py:17
  313.2 15.0 %collective-permute-done.9 = bf16[1024,384]{1,0:T(8,128)(2,1)S(1)} collective-permute-done((bf16[1024,384]{1,0:T(8,128)(2,1)S(1)}, bf16[1024,384]{1,0:T(8,128)(2,1)S(1)}, u32[]{:S(2)}, u32[]{:S(2)}) %collective-permute-start.9) | collective-permute-done | bytes 786464 | tf_op jit(solution)/shard_map/ppermute | solution.py:17
  328.2 2.7 fusion.1
  330.9 7.5 %all-to-all-start.6 = ((bf16[8,128,384]{2,1,0:T(8,128)(2,1)}), bf16[8,128,384]{2,1,0:T(8,128)(2,1)}, u32[]{:S(2)}, u32[]{:S(2)}) async-start(bf16[8,128,384]{2,1,0:T(8,128)(2,1)} %bitcast.118), calls=%async_computation.6 | async-start | bytes 1572864 | tf_op jit(solution)/shard_map/all_to_all | solution.py:236
  340.6 7.9 %collective-permute-start.16 = (bf16[1024,384]{1,0:T(8,128)(2,1)S(1)}, bf16[1024,384]{1,0:T(8,128)(2,1)S(1)}, u32[]{:S(2)}, u32[]{:S(2)}) collective-permute-start(bf16[1024,384]{1,0:T(8,128)(2,1)S(1)} %get-tuple-element.12), channel_id=1, source_target_pairs={{8,0},{16,8},{24,16},{32,24},{40,32},{48,40},{56,48},{64,56},{72,6... | collective-permute-start | bytes 2359304 | tf_op jit(solution)/shard_map/ppermute | solution.py:17
  350.5 13.8 %collective-permute-done.17 = bf16[1024,384]{1,0:T(8,128)(2,1)S(1)} collective-permute-done((bf16[1024,384]{1,0:T(8,128)(2,1)S(1)}, bf16[1024,384]{1,0:T(8,128)(2,1)S(1)}, u32[]{:S(2)}, u32[]{:S(2)}) %collective-permute-start.17) | collective-permute-done | bytes 786464 | tf_op jit(solution)/shard_map/ppermute | solution.py:17
  364.3 4.9 %collective-permute-done.16 = bf16[1024,384]{1,0:T(8,128)(2,1)S(1)} collective-permute-done((bf16[1024,384]{1,0:T(8,128)(2,1)S(1)}, bf16[1024,384]{1,0:T(8,128)(2,1)S(1)}, u32[]{:S(2)}, u32[]{:S(2)}) %collective-permute-start.16) | collective-permute-done | bytes 786464 | tf_op jit(solution)/shard_map/ppermute | solution.py:17
  369.2 2.8 fusion
  371.9 6.1 %all-to-all-start.7 = ((bf16[8,128,384]{2,1,0:T(8,128)(2,1)}), bf16[8,128,384]{2,1,0:T(8,128)(2,1)S(1)}, u32[]{:S(2)}, u32[]{:S(2)}) async-start(bf16[8,128,384]{2,1,0:T(8,128)(2,1)} %bitcast.37), calls=%async_computation.7 | async-start | bytes 1572864 | tf_op jit(solution)/shard_map/all_to_all | solution.py:237
  383.3 3.4 all-to-all-done.7
  (90 shorter events, 69.4 us)
Async XLA Ops:
  0.6 8.1 %copy-start.2 = (bf16[128,3072]{1,0:T(8,128)(2,1)S(1)}, bf16[128,3072]{1,0:T(8,128)(2,1)}, u32[]{:S(2)}) copy-start(bf16[128,3072]{1,0:T(8,128)(2,1)} %param.6) | copy-start | bytes 2359300
  3.0 17.2 %all-to-all-start.3 = ((bf16[128,8,384]{0,2,1:T(8,128)(2,1)}), bf16[128,8,384]{0,2,1:T(8,128)(2,1)S(1)}, u32[]{:S(2)}, u32[]{:S(2)}) async-start(bf16[128,8,384]{0,2,1:T(8,128)(2,1)} %bitcast.17), calls=%async_computation.3 | async-start | bytes 1572864 | tf_op jit(solution)/shard_map/all_to_all | solution.py:142
  20.2 15.8 %all-to-all-start.2 = ((bf16[128,8,384]{0,2,1:T(8,128)(2,1)}), bf16[128,8,384]{0,2,1:T(8,128)(2,1)S(1)}, u32[]{:S(2)}, u32[]{:S(2)}) async-start(bf16[128,8,384]{0,2,1:T(8,128)(2,1)} %bitcast.4), calls=%async_computation.2 | async-start | bytes 1572864 | tf_op jit(solution)/shard_map/all_to_all | solution.py:141
  25.2 12.1 %copy-start.4 = (s32[8]{0:T(128)}, s32[8]{0:T(128)S(1)}, u32[]{:S(2)}) copy-start(s32[8]{0:T(128)S(1)} %iota_add_fusion) | copy-start | bytes 100
  36.4 5.6 %copy-start.3 = (bf16[128,3072]{1,0:T(8,128)(2,1)S(1)}, bf16[128,3072]{1,0:T(8,128)(2,1)}, u32[]{:S(2)}) copy-start(bf16[128,3072]{1,0:T(8,128)(2,1)} %param.5) | copy-start | bytes 2359300
  37.9 1.8 collective-permute-start.2
  40.4 11.2 %collective-permute-start.3 = (bf16[2,2,128,3,128]{4,1,2,3,0:T(2,128)(2,1)S(1)}, bf16[2,2,128,3,128]{4,1,2,3,0:T(2,128)(2,1)S(1)}, u32[]{:S(2)}, u32[]{:S(2)}) collective-permute-start(bf16[2,2,128,3,128]{4,1,2,3,0:T(2,128)(2,1)S(1)} %fusion.20), channel_id=1, source_target_pairs={{0,16},{8,24},{16,0},{24,8},{32,48},{40,56},{48,32},{56,40},{64,80... | collective-permute-start | bytes 1179656 | tf_op jit(solution)/shard_map/ppermute | solution.py:27
  43.0 42.1 %all-to-all-start = ((bf16[128,8,384]{2,0,1:T(8,128)(2,1)}), bf16[128,8,384]{2,0,1:T(8,128)(2,1)}, u32[]{:S(2)}, u32[]{:S(2)}) async-start(bf16[128,8,384]{2,0,1:T(8,128)(2,1)} %bitcast.99), calls=%async_computation | async-start | bytes 1572864 | tf_op jit(solution)/shard_map/all_to_all | solution.py:140
  52.4 12.9 %collective-permute-start.4 = (bf16[2,2,128,3,128]{4,1,2,3,0:T(2,128)(2,1)S(1)}, bf16[2,2,128,3,128]{4,1,2,3,0:T(2,128)(2,1)S(1)}, u32[]{:S(2)}, u32[]{:S(2)}) collective-permute-start(bf16[2,2,128,3,128]{4,1,2,3,0:T(2,128)(2,1)S(1)} %fusion.26), channel_id=1, source_target_pairs={{0,32},{8,40},{16,48},{24,56},{32,0},{40,8},{48,16},{56,24},{64,96... | collective-permute-start | bytes 1179656 | tf_op jit(solution)/shard_map/ppermute | solution.py:27
  56.1 72.3 %collective-permute-start.1 = (bf16[1024,384]{1,0:T(8,128)(2,1)S(1)}, bf16[1024,384]{1,0:T(8,128)(2,1)}, u32[]{:S(2)}, u32[]{:S(2)}) collective-permute-start(bf16[1024,384]{1,0:T(8,128)(2,1)S(1)} %bitcast.110), channel_id=1, source_target_pairs={{8,0},{16,8},{24,16},{32,24},{40,32},{48,40},{56,48},{64,56},{72,6... | collective-permute-start | bytes 2359304 | tf_op jit(solution)/shard_map/ppermute | solution.py:17
  58.0 70.4 %collective-permute-start = (bf16[1024,384]{1,0:T(8,128)(2,1)S(1)}, bf16[1024,384]{1,0:T(8,128)(2,1)}, u32[]{:S(2)}, u32[]{:S(2)}) collective-permute-start(bf16[1024,384]{1,0:T(8,128)(2,1)S(1)} %bitcast.111), channel_id=1, source_target_pairs={{0,8},{8,16},{16,24},{24,32},{32,40},{40,48},{48,56},{56,64},{64,7... | collective-permute-start | bytes 2359304 | tf_op jit(solution)/shard_map/ppermute | solution.py:17
  65.8 15.9 %collective-permute-start.5 = (bf16[2,2,128,3,128]{4,1,2,3,0:T(2,128)(2,1)S(1)}, bf16[2,2,128,3,128]{4,1,2,3,0:T(2,128)(2,1)}, u32[]{:S(2)}, u32[]{:S(2)}) collective-permute-start(bf16[2,2,128,3,128]{4,1,2,3,0:T(2,128)(2,1)S(1)} %add.71), channel_id=1, source_target_pairs={{0,64},{8,72},{16,80},{24,88},{32,96},{40,104},{48,112},{56,120},{... | collective-permute-start | bytes 1179656 | tf_op jit(solution)/shard_map/ppermute | solution.py:27
  67.7 62.3 %collective-permute-start.8 = (bf16[1024,384]{1,0:T(8,128)(2,1)S(1)}, bf16[1024,384]{1,0:T(8,128)(2,1)S(1)}, u32[]{:S(2)}, u32[]{:S(2)}) collective-permute-start(bf16[1024,384]{1,0:T(8,128)(2,1)S(1)} %bitcast.113), channel_id=1, source_target_pairs={{8,0},{16,8},{24,16},{32,24},{40,32},{48,40},{56,48},{64,56},{72,6... | collective-permute-start | bytes 2359304 | tf_op jit(solution)/shard_map/ppermute | solution.py:17
  69.6 60.4 %collective-permute-start.7 = (bf16[1024,384]{1,0:T(8,128)(2,1)S(1)}, bf16[1024,384]{1,0:T(8,128)(2,1)}, u32[]{:S(2)}, u32[]{:S(2)}) collective-permute-start(bf16[1024,384]{1,0:T(8,128)(2,1)S(1)} %bitcast.114), channel_id=1, source_target_pairs={{0,8},{8,16},{16,24},{24,32},{32,40},{40,48},{48,56},{56,64},{64,7... | collective-permute-start | bytes 2359304 | tf_op jit(solution)/shard_map/ppermute | solution.py:17
  83.1 48.4 %collective-permute-start.6 = (bf16[2,2,128,3,128]{4,1,2,3,0:T(2,128)(2,1)S(1)}, bf16[2,2,128,3,128]{4,1,2,3,0:T(2,128)(2,1)S(1)}, u32[]{:S(2)}, u32[]{:S(2)}) collective-permute-start(bf16[2,2,128,3,128]{4,1,2,3,0:T(2,128)(2,1)S(1)} %add.72), channel_id=1, source_target_pairs={{0,128},{8,136},{16,144},{24,152},{32,160},{40,168},{48,176},{56,1... | collective-permute-start | bytes 1179656 | tf_op jit(solution)/shard_map/ppermute | solution.py:27
  85.1 57.8 %all-to-all-start.1 = ((bf16[128,8,384]{2,0,1:T(8,128)(2,1)}), bf16[128,8,384]{2,0,1:T(8,128)(2,1)}, u32[]{:S(2)}, u32[]{:S(2)}) async-start(bf16[128,8,384]{2,0,1:T(8,128)(2,1)} %bitcast.98), calls=%async_computation.1 | async-start | bytes 1572864 | tf_op jit(solution)/shard_map/all_to_all | solution.py:143
  182.6 2.4 collective-permute-start.11
  185.4 19.7 %collective-permute-start.12 = (f32[2,2,128,3,128]{4,1,2,3,0:T(2,128)S(1)}, f32[2,2,128,3,128]{4,1,2,3,0:T(2,128)S(1)}, u32[]{:S(2)}, u32[]{:S(2)}) collective-permute-start(f32[2,2,128,3,128]{4,1,2,3,0:T(2,128)S(1)} %add.76), channel_id=1, source_target_pairs={{0,16},{8,24},{16,0},{24,8},{32,48},{40,56},{48,32},{56,40},{64,80... | collective-permute-start | bytes 2359304 | tf_op jit(solution)/shard_map/ppermute | solution.py:27
  205.5 20.3 %collective-permute-start.13 = (f32[2,2,128,3,128]{4,1,2,3,0:T(2,128)S(1)}, f32[2,2,128,3,128]{4,1,2,3,0:T(2,128)S(1)}, u32[]{:S(2)}, u32[]{:S(2)}) collective-permute-start(f32[2,2,128,3,128]{4,1,2,3,0:T(2,128)S(1)} %add.77), channel_id=1, source_target_pairs={{0,32},{8,40},{16,48},{24,56},{32,0},{40,8},{48,16},{56,24},{64,96... | collective-permute-start | bytes 2359304 | tf_op jit(solution)/shard_map/ppermute | solution.py:27
  208.1 58.4 %all-to-all-start.4 = ((bf16[8,128,384]{2,1,0:T(8,128)(2,1)}), bf16[8,128,384]{2,1,0:T(8,128)(2,1)S(1)}, u32[]{:S(2)}, u32[]{:S(2)}) async-start(bf16[8,128,384]{2,1,0:T(8,128)(2,1)} %bitcast.27), calls=%async_computation.4 | async-start | bytes 1572864 | tf_op jit(solution)/shard_map/all_to_all | solution.py:234
  226.2 36.8 %collective-permute-start.14 = (f32[2,2,128,3,128]{4,1,2,3,0:T(2,128)S(1)}, f32[2,2,128,3,128]{4,1,2,3,0:T(2,128)S(1)}, u32[]{:S(2)}, u32[]{:S(2)}) collective-permute-start(f32[2,2,128,3,128]{4,1,2,3,0:T(2,128)S(1)} %add.78), channel_id=1, source_target_pairs={{0,64},{8,72},{16,80},{24,88},{32,96},{40,104},{48,112},{56,120},{... | collective-permute-start | bytes 2359304 | tf_op jit(solution)/shard_map/ppermute | solution.py:27
  264.4 30.5 %collective-permute-start.15 = (f32[2,2,128,3,128]{4,1,2,3,0:T(2,128)}, f32[2,2,128,3,128]{4,1,2,3,0:T(2,128)}, u32[]{:S(2)}, u32[]{:S(2)}) collective-permute-start(f32[2,2,128,3,128]{4,1,2,3,0:T(2,128)} %add.79), channel_id=1, source_target_pairs={{0,128},{8,136},{16,144},{24,152},{32,160},{40,168},{48,176},{56,1... | collective-permute-start | bytes 2359304 | tf_op jit(solution)/shard_map/ppermute | solution.py:27
  266.5 64.4 %all-to-all-start.5 = ((bf16[8,128,384]{2,1,0:T(8,128)(2,1)}), bf16[8,128,384]{2,1,0:T(8,128)(2,1)}, u32[]{:S(2)}, u32[]{:S(2)}) async-start(bf16[8,128,384]{2,1,0:T(8,128)(2,1)} %bitcast.124), calls=%async_computation.5 | async-start | bytes 1572864 | tf_op jit(solution)/shard_map/all_to_all | solution.py:235
  274.5 38.7 %collective-permute-start.10 = (bf16[1024,384]{1,0:T(8,128)(2,1)S(1)}, bf16[1024,384]{1,0:T(8,128)(2,1)S(1)}, u32[]{:S(2)}, u32[]{:S(2)}) collective-permute-start(bf16[1024,384]{1,0:T(8,128)(2,1)S(1)} %get-tuple-element.15), channel_id=1, source_target_pairs={{0,8},{8,16},{16,24},{24,32},{32,40},{40,48},{48,56},{56,64},{64,7... | collective-permute-start | bytes 2359304 | tf_op jit(solution)/shard_map/ppermute | solution.py:17
  276.4 51.8 %collective-permute-start.9 = (bf16[1024,384]{1,0:T(8,128)(2,1)S(1)}, bf16[1024,384]{1,0:T(8,128)(2,1)S(1)}, u32[]{:S(2)}, u32[]{:S(2)}) collective-permute-start(bf16[1024,384]{1,0:T(8,128)(2,1)S(1)} %get-tuple-element.14), channel_id=1, source_target_pairs={{8,0},{16,8},{24,16},{32,24},{40,32},{48,40},{56,48},{64,56},{72,6... | collective-permute-start | bytes 2359304 | tf_op jit(solution)/shard_map/ppermute | solution.py:17
  287.0 10.6 %copy-start.5 = (s32[8]{0:T(128)S(1)}, s32[8]{0:T(128)}, u32[]{:S(2)}) copy-start(s32[8]{0:T(128)} %copy-done.4) | copy-start | bytes 100
  296.7 0.9 copy-start
  330.9 41.1 %all-to-all-start.6 = ((bf16[8,128,384]{2,1,0:T(8,128)(2,1)}), bf16[8,128,384]{2,1,0:T(8,128)(2,1)}, u32[]{:S(2)}, u32[]{:S(2)}) async-start(bf16[8,128,384]{2,1,0:T(8,128)(2,1)} %bitcast.118), calls=%async_computation.6 | async-start | bytes 1572864 | tf_op jit(solution)/shard_map/all_to_all | solution.py:236
  338.4 10.1 %copy-start.1 = (f32[2,2,128,3,128]{4,1,2,3,0:T(2,128)S(1)}, f32[2,2,128,3,128]{4,1,2,3,0:T(2,128)}, u32[]{:S(2)}) copy-start(f32[2,2,128,3,128]{4,1,2,3,0:T(2,128)} %copy-done) | copy-start | bytes 2359300
  338.5 25.8 %collective-permute-start.17 = (bf16[1024,384]{1,0:T(8,128)(2,1)S(1)}, bf16[1024,384]{1,0:T(8,128)(2,1)S(1)}, u32[]{:S(2)}, u32[]{:S(2)}) collective-permute-start(bf16[1024,384]{1,0:T(8,128)(2,1)S(1)} %get-tuple-element.13), channel_id=1, source_target_pairs={{0,8},{8,16},{16,24},{24,32},{32,40},{40,48},{48,56},{56,64},{64,7... | collective-permute-start | bytes 2359304 | tf_op jit(solution)/shard_map/ppermute | solution.py:17
  340.6 28.6 %collective-permute-start.16 = (bf16[1024,384]{1,0:T(8,128)(2,1)S(1)}, bf16[1024,384]{1,0:T(8,128)(2,1)S(1)}, u32[]{:S(2)}, u32[]{:S(2)}) collective-permute-start(bf16[1024,384]{1,0:T(8,128)(2,1)S(1)} %get-tuple-element.12), channel_id=1, source_target_pairs={{8,0},{16,8},{24,16},{32,24},{40,32},{48,40},{56,48},{64,56},{72,6... | collective-permute-start | bytes 2359304 | tf_op jit(solution)/shard_map/ppermute | solution.py:17
  371.9 14.8 %all-to-all-start.7 = ((bf16[8,128,384]{2,1,0:T(8,128)(2,1)}), bf16[8,128,384]{2,1,0:T(8,128)(2,1)S(1)}, u32[]{:S(2)}, u32[]{:S(2)}) async-start(bf16[8,128,384]{2,1,0:T(8,128)(2,1)} %bitcast.37), calls=%async_computation.7 | async-start | bytes 1572864 | tf_op jit(solution)/shard_map/all_to_all | solution.py:237
